TPU v7x, 256 devices: a whole 4x4x8 slice. The times are simulated.
256 devices in a mesh: dom: 32 (over x, z), cls: 4 (over y), own: 2 (over core).
Axes of the slice: x: 4, y: 4, z: 8, core: 2. Of those that a mesh axis runs over, the one named last changes fastest.
Arguments:
- images: bfloat16 [12288, 4096], P('dom'), may hold values from -6 to 6
- templates: bfloat16 [4, 1152, 4096], P('cls', ('dom', 'own')), may hold values from -0.09375 to 0.09375
- offsets: int32 [12288, 4], P('dom'), may hold values from 0 to 63
- groups: int32 [12288], P('dom'), may hold values from 0 to 15
- prior_block: int32 [12288], P('dom'), may hold values from 0 to 17
- group_weight: float32 [16], replicated, may hold values from 0.5 to 64
- class_log_prior: float32 [4], replicated, may hold values from -1 to 1
Outputs:
- class_post: float32 [12288, 4], P('dom', 'cls')
- class_sums: float32 [4, 1152, 4096], P('cls', ('dom', 'own'))
All inputs are finite; a program needn't handle non-finite values.
Results may differ from a plain program's by a relative error of at most 0.0065.
Values may be sent and summed in bfloat16 or wider, within the bound.
No kernel may reach another device: no remote copies, remote signals or barrier semaphores. Data moves between devices by JAX's collectives and lax.ppermute only.
A program may use at most 128 MiB of HBM per device.

v0:
```python
import jax
import jax.numpy as jnp
from jax import lax
from jax.sharding import PartitionSpec as P

SIDE = 64
ORIENT_PER_BLOCK = 64


BLOCK_PRIOR_GAIN = 1.5


def roll_image(doubled_rows, shift_rows):

    def take_rows(start_row):
        return lax.dynamic_slice_in_dim(doubled_rows, start_row, SIDE, 0)

    return jax.vmap(take_rows)(shift_rows)


def shards(images, templates, offsets, groups, prior_block, group_weight, class_log_prior):
    rows_local = images.shape[0]
    pixels = images.shape[1]
    shift_count = offsets.shape[1]
    image_grid = images.reshape(rows_local, SIDE, SIDE)
    doubled = jnp.concatenate([image_grid, image_grid], axis=1)
    shifted = jax.vmap(roll_image)(doubled, offsets).reshape(rows_local * shift_count, pixels)
    onehot = (
        groups[:, None] == jnp.arange(group_weight.shape[0], dtype=jnp.int32)[None, :]
    ).astype(jnp.float32)
    noise_variance = jnp.dot(onehot, group_weight, precision=lax.Precision.HIGHEST)
    noise_weight_rows = jnp.repeat(noise_variance, shift_count)
    log_prior_rows = jnp.repeat(prior_block, shift_count)
    class_offset_bias = class_log_prior[lax.axis_index("cls")]
    per_device = templates.shape[1]
    owners = lax.axis_size("own")
    owner = lax.axis_index("own")
    template_piece = lax.all_gather(templates[0], "dom", axis=0, tiled=True)
    cross_correlation = lax.dot_general(
        shifted, template_piece, (((1,), (1,)), ((), ())), preferred_element_type=jnp.float32
    )
    signal_energy = jnp.sum(jnp.square(template_piece.astype(jnp.float32)), axis=1)
    position = jnp.arange(template_piece.shape[0], dtype=jnp.int32)
    orientation_index = (
        position // per_device * (per_device * owners) + owner * per_device + position % per_device
    )
    prior_gain = BLOCK_PRIOR_GAIN * (
        orientation_index[None, :] // ORIENT_PER_BLOCK == log_prior_rows[:, None]
    ).astype(jnp.float32)
    match_score = (
        noise_weight_rows[:, None] * (cross_correlation - 0.5 * signal_energy[None, :])
        + class_offset_bias
        + prior_gain
    )
    orient_local = match_score.shape[1]
    grouped = match_score.reshape(rows_local, shift_count * orient_local)
    local_peak = jnp.max(grouped, axis=1)
    peak_value = lax.pmax(local_peak, ("cls", "own"))
    exps = jnp.exp(grouped - peak_value[:, None])
    mass_total = lax.psum(jnp.sum(exps, axis=1), ("cls", "own"))
    posterior = exps / mass_total[:, None]
    class_part = jnp.sum(posterior, axis=1)
    class_post = lax.psum(class_part, "own")[:, None]
    weight16 = posterior.reshape(rows_local * shift_count, orient_local).astype(jnp.bfloat16)
    partial_term = lax.dot_general(
        weight16, shifted, (((0,), (0,)), ((), ())), preferred_element_type=jnp.float32
    )
    class_sums = lax.psum_scatter(partial_term, "dom", scatter_dimension=0, tiled=True)
    return (class_post, class_sums[None])


def solution(mesh):
    placed = (
        P("dom", None),
        P("cls", ("dom", "own"), None),
        P("dom", None),
        P("dom"),
        P("dom"),
        P(),
        P(),
    )
    return jax.shard_map(
        shards,
        mesh=mesh,
        in_specs=placed,
        out_specs=(P("dom", "cls"), P("cls", ("dom", "own"), None)),
        check_vma=False,
    )
```

profile of v0, /device:TPU:1, one launch (start us, length us, event | category | flops | bytes accessed | tf_op | source)
XLA Modules:
  0.0 495.6 jit_solution(12178631057075051216)
XLA Ops:
  7.2 1.9 copy.28
  9.2 3.4 copy.23
  12.6 4.7 copy.24
  17.4 0.1 copy.26
  17.5 0.1 reshape.84
  17.6 11.3 %pad_maximum_fusion = bf16[384,128,64]{2,0,1:T(8,128)(2,1)} fusion(bf16[384,64,64]{2,0,1:T(8,128)(2,1)} %copy.24), kind=kLoop, calls=%fused_computation.1 | loop fusion | flops 3145728 | bytes 9437184 | tf_op jit(solution)/shard_map/concatenate | solution.py:26
  28.9 99.5 %gather_fusion = bf16[1536,64,64]{2,0,1:T(8,128)(2,1)} fusion(bf16[384,128,64]{2,0,1:T(8,128)(2,1)} %pad_maximum_fusion, s32[1536]{0:T(1024)S(1)} %reshape.84), kind=kCustom, calls=%fused_computation | custom fusion | bytes 25184256 | tf_op jit(solution)/shard_map/vmap(vmap())/gather | solution.py:16
  128.5 23.3 %copy.27 = bf16[1536,64,64]{0,2,1:T(8,128)(2,1)} copy(bf16[1536,64,64]{2,0,1:T(8,128)(2,1)} %gather_fusion) | data formatting | bytes 25165824 | tf_op jit(solution)/shard_map/vmap(vmap())/gather | solution.py:16
  151.8 0.3 convolution_reduce_fusion
  152.2 0.1 mul.40
  152.5 0.7 eq.34
  153.2 0.6 dynamic_slice.3
  153.9 8.8 %multiply_reduce_fusion = f32[576]{0:T(1024)S(1)} fusion(bf16[1,576,4096]{2,0,1:T(2,128)(2,1)} %all-gather.3.cloned.1.call-done), kind=kLoop, calls=%fused_computation.2 | loop fusion | flops 7077312 | bytes 4720896 | tf_op jit(solution)/shard_map/reduce_sum | solution.py:42
  162.7 19.7 %fusion.30 = (f32[1536]{0:T(1024)}, f32[1536,576]{0,1:T(8,128)S(1)}) fusion(s32[1536]{0:T(1024)S(1)} %copy-done.2, s32[576]{0:T(1024)S(1)} %add_select_fusion, f32[]{:T(128)} %bitcast.4, f32[576]{0:T(1024)S(1)} %broadcast_multiply_fusion, bf16[1536,4096]{0,1:T(8,128)(2,1)} %bitcast.28, bf16[1,576,4096]{2,0,1:T(2,128)(2,1)S(1)} %copy-done.1, f32[1536]{0:T(1024)S(1)} %mul.40), kind=kOutput, calls=%fused_computation.45 | convolution fusion | flops 7253948928 | bytes 20863492 | tf_op jit(solution)/shard_map/dot_general | solution.py:39
  182.5 1.6 reduce_max.14
  184.0 1.1 reduce_max.18
  185.1 15.3 %pmax.7 = f32[384]{0:T(512)S(1)} all-reduce(f32[384]{0:T(512)S(1)} %reduce_max.18), channel_id=1, replica_groups=mesh['dom'=32,'cls'=4,'own'=2] {'cls','own'}, use_global_device_ids=true, to_apply=%region_3.4 | all-reduce | flops 384 | bytes 3072 | tf_op jit(solution)/shard_map/pmax | solution.py:58
  200.4 0.8 sub.39
  201.2 1.1 sub.40
  202.2 1.1 fusion.6
  203.3 1.6 reduce_sum.36
  204.9 1.1 reduce_sum.44
  206.0 13.7 %psum.14 = f32[384]{0:T(512)} all-reduce(f32[384]{0:T(512)S(1)} %reduce_sum.44), channel_id=1, replica_groups=mesh['dom'=32,'cls'=4,'own'=2] {'cls','own'}, use_global_device_ids=true, to_apply=%region_6.7 | all-reduce | flops 384 | bytes 3072 | tf_op jit(solution)/shard_map/psum | solution.py:60
  219.7 1.5 div.41
  221.1 1.7 div.42
  222.8 12.8 %fusion.8 = f32[576,4096]{1,0:T(8,128)} fusion(bf16[1536,4096]{0,1:T(8,128)(2,1)} %bitcast.29, f32[1536,576]{0,1:T(8,128)S(1)} %get-tuple-element.11, f32[1536]{0:T(1024)} %div.42, f32[1536]{0:T(1024)S(1)} %sub.40), kind=kOutput, calls=%fused_computation.10 | convolution fusion | flops 7250411520 | bytes 25571328 | tf_op jit(solution)/shard_map/dot_general | solution.py:65
  235.6 147.0 %fusion = f32[24,4096]{1,0:T(8,128)} fusion(f32[576,4096]{1,0:T(8,128)} %fusion.8), kind=kCustom, calls=%all-reduce-scatter | all-reduce-scatter fusion | flops 3145729 | bytes 9831424
  382.5 2.8 collective-permute-start
  385.3 2.0 collective-permute-start.1
  387.3 1.8 slice.5
  389.1 2.0 collective-permute-start.7
  391.2 0.6 dynamic-slice.4
  392.4 4.3 collective-permute-start.2
  396.7 6.1 %collective-permute-start.3 = (f32[24,4096]{1,0:T(8,128)}, f32[24,4096]{1,0:T(8,128)}, u32[]{:S(2)}, u32[]{:S(2)}) collective-permute-start(f32[24,4096]{1,0:T(8,128)} %fusion), channel_id=1, source_target_pairs={{0,32},{8,40},{16,48},{24,56},{32,64},{40,72},{48,80},{56,88},{64,... | collective-permute-start | bytes 1179656
  402.8 7.3 %collective-permute-done.7 = f32[18,4096]{1,0:T(8,128)} collective-permute-done((f32[18,4096]{1,0:T(8,128)}, f32[18,4096]{1,0:T(8,128)}, u32[]{:S(2)}, u32[]{:S(2)}) %collective-permute-start.7) | collective-permute-done | bytes 294944
  410.1 2.0 collective-permute-start.4
  412.2 2.0 collective-permute-start.5
  414.2 2.1 collective-permute-start.6
  416.3 1.9 fusion.11
  418.2 0.9 reduce_sum.46
  419.0 0.1 reduce_sum.47
  419.2 13.3 %psum.15 = f32[384,1]{0,1:T(1,128)} all-reduce(f32[384,1]{0,1:T(1,128)S(1)} %broadcast_in_dim.25), channel_id=1, replica_groups=mesh['dom'=32,'cls'=4,'own'=2] {'own'}, use_global_device_ids=true, to_apply=%region_9.10 | all-reduce | flops 384 | bytes 3072 | tf_op jit(solution)/shard_map/psum | solution.py:63
  432.5 5.4 %collective-permute-done.3 = f32[24,4096]{1,0:T(8,128)} collective-permute-done((f32[24,4096]{1,0:T(8,128)}, f32[24,4096]{1,0:T(8,128)}, u32[]{:S(2)}, u32[]{:S(2)}) %collective-permute-start.3) | collective-permute-done | bytes 393248
  437.9 7.2 %collective-permute-done.4 = f32[24,4096]{1,0:T(8,128)} collective-permute-done((f32[24,4096]{1,0:T(8,128)}, f32[24,4096]{1,0:T(8,128)}, u32[]{:S(2)}, u32[]{:S(2)}) %collective-permute-start.4) | collective-permute-done | bytes 393248
  445.1 16.0 %collective-permute-done.5 = f32[24,4096]{1,0:T(8,128)} collective-permute-done((f32[24,4096]{1,0:T(8,128)}, f32[24,4096]{1,0:T(8,128)}, u32[]{:S(2)}, u32[]{:S(2)}) %collective-permute-start.5) | collective-permute-done | bytes 393248
  461.1 8.7 %collective-permute-done.6 = f32[24,4096]{1,0:T(8,128)} collective-permute-done((f32[24,4096]{1,0:T(8,128)}, f32[24,4096]{1,0:T(8,128)}, u32[]{:S(2)}, u32[]{:S(2)}) %collective-permute-start.6) | collective-permute-done | bytes 393248
  469.8 17.9 %concatenate.11 = f32[210,4096]{1,0:T(8,128)S(1)} concatenate(f32[18,4096]{1,0:T(8,128)} %collective-permute-done.7, f32[24,4096]{1,0:T(8,128)} %collective-permute-done.6, f32[24,4096]{1,0:T(8,128)} %collective-permute-done.5, f32[24,4096]{1,0:T(8,128)} %collective-permute-done.4, f32[24,4096]{1,0:T(8,128)} %collective-permute-done.3, f32[24,4096]{1,0:T(8,128)} %collective-permute-done.2, ...), dimensions={0} | concatenate | bytes 6881280
  487.7 1.0 copy.29
  (29 shorter events, 0.4 us)
Async XLA Ops:
  7.2 144.6 %copy-start = (f32[16]{0:T(128)S(1)}, f32[16]{0:T(128)}, u32[]{:S(2)}) copy-start(f32[16]{0:T(128)} %param.12) | copy-start | bytes 196
  7.2 146.7 %all-gather.3.cloned.1.call-start = ((), (), s32[]{:S(2)}) async-start(), calls=%async_computation | async-start | bytes 9732096 | tf_op jit(solution)/shard_map/all_gather | solution.py:38
  12.6 4.7 copy-start.3
  128.4 23.3 %copy-start.6 = (s32[384]{0:T(512)S(1)}, s32[384]{0:T(512)}, u32[]{:S(2)}) copy-start(s32[384]{0:T(512)} %param.10) | copy-start | bytes 4612
  128.4 23.9 %copy-start.4 = (s32[384]{0:T(512)S(1)}, s32[384]{0:T(512)}, u32[]{:S(2)}) copy-start(s32[384]{0:T(512)} %param.11) | copy-start | bytes 4612
  128.5 24.8 %copy-start.7 = (f32[4]{0:T(128)S(1)}, f32[4]{0:T(128)}, u32[]{:S(2)}) copy-start(f32[4]{0:T(128)} %param.13) | copy-start | bytes 52
  153.9 8.8 %copy-start.1 = (bf16[1,576,4096]{2,0,1:T(2,128)(2,1)S(1)}, bf16[1,576,4096]{2,0,1:T(2,128)(2,1)}, u32[]{:S(2)}) copy-start(bf16[1,576,4096]{2,0,1:T(2,128)(2,1)} %all-gather.3.cloned.1.call-done) | copy-start | bytes 14155780
  153.9 8.8 %copy-start.2 = (s32[1536]{0:T(1024)S(1)}, s32[1536]{0:T(1024)}, u32[]{:S(2)}) copy-start(s32[1536]{0:T(1024)} %eq.34) | copy-start | bytes 18436
  235.6 155.6 %copy-start.5 = (u32[256]{0:T(256)S(1)}, u32[256]{0:T(256)}, u32[]{:S(2)}) copy-start(u32[256]{0:T(256)} %constant.85) | copy-start | bytes 3076
  382.5 29.6 %collective-permute-start = (f32[24,4096]{1,0:T(8,128)}, f32[24,4096]{1,0:T(8,128)}, u32[]{:S(2)}, u32[]{:S(2)}) collective-permute-start(f32[24,4096]{1,0:T(8,128)} %fusion), channel_id=1, source_target_pairs={{0,8},{8,16},{16,24},{24,32},{32,40},{40,48},{48,56},{56,64},{64,7... | collective-permute-start | bytes 1179656
  385.3 28.9 %collective-permute-start.1 = (f32[24,4096]{1,0:T(8,128)}, f32[24,4096]{1,0:T(8,128)}, u32[]{:S(2)}, u32[]{:S(2)}) collective-permute-start(f32[24,4096]{1,0:T(8,128)} %fusion), channel_id=1, source_target_pairs={{0,16},{8,24},{16,32},{24,40},{32,48},{40,56},{48,64},{56,72},{64,... | collective-permute-start | bytes 1179656
  389.1 21.0 %collective-permute-start.7 = (f32[18,4096]{1,0:T(8,128)}, f32[18,4096]{1,0:T(8,128)}, u32[]{:S(2)}, u32[]{:S(2)}) collective-permute-start(f32[18,4096]{1,0:T(8,128)} %slice.5), channel_id=1, source_target_pairs={{0,64},{8,72},{16,80},{24,88},{32,96},{40,104},{48,112},{56,120},{... | collective-permute-start | bytes 884744
  392.4 40.1 %collective-permute-start.2 = (f32[24,4096]{1,0:T(8,128)}, f32[24,4096]{1,0:T(8,128)}, u32[]{:S(2)}, u32[]{:S(2)}) collective-permute-start(f32[24,4096]{1,0:T(8,128)} %fusion), channel_id=1, source_target_pairs={{0,24},{8,32},{16,40},{24,48},{32,56},{40,64},{48,72},{56,80},{64,... | collective-permute-start | bytes 1179656
  396.7 41.2 %collective-permute-start.3 = (f32[24,4096]{1,0:T(8,128)}, f32[24,4096]{1,0:T(8,128)}, u32[]{:S(2)}, u32[]{:S(2)}) collective-permute-start(f32[24,4096]{1,0:T(8,128)} %fusion), channel_id=1, source_target_pairs={{0,32},{8,40},{16,48},{24,56},{32,64},{40,72},{48,80},{56,88},{64,... | collective-permute-start | bytes 1179656
  410.1 35.0 %collective-permute-start.4 = (f32[24,4096]{1,0:T(8,128)}, f32[24,4096]{1,0:T(8,128)}, u32[]{:S(2)}, u32[]{:S(2)}) collective-permute-start(f32[24,4096]{1,0:T(8,128)} %fusion), channel_id=1, source_target_pairs={{0,40},{8,48},{16,56},{24,64},{32,72},{40,80},{48,88},{56,96},{64,... | collective-permute-start | bytes 1179656
  412.2 49.0 %collective-permute-start.5 = (f32[24,4096]{1,0:T(8,128)}, f32[24,4096]{1,0:T(8,128)}, u32[]{:S(2)}, u32[]{:S(2)}) collective-permute-start(f32[24,4096]{1,0:T(8,128)} %fusion), channel_id=1, source_target_pairs={{0,48},{8,56},{16,64},{24,72},{32,80},{40,88},{48,96},{56,104},{64... | collective-permute-start | bytes 1179656
  414.2 55.6 %collective-permute-start.6 = (f32[24,4096]{1,0:T(8,128)}, f32[24,4096]{1,0:T(8,128)}, u32[]{:S(2)}, u32[]{:S(2)}) collective-permute-start(f32[24,4096]{1,0:T(8,128)} %fusion), channel_id=1, source_target_pairs={{0,56},{8,64},{16,72},{24,80},{32,88},{40,96},{48,104},{56,112},{6... | collective-permute-start | bytes 1179656
Sparse Core Ops, SparseCore 0:
  11.2 106.8 all-gather.2
where the time goes:
time: 501 us; the launch traced here: 496 us
  blocking collectives  189 us (38%)
  local copies, waits for them, and re-layouts  165 us (33%)
  waiting for transfers between devices  44.6 us (9%)
  matrix products  32.8 us (7%)
  other arithmetic  25.4 us (5%)
  starting transfers between devices  23.4 us (5%)
  between operations  14.9 us (3%)
    unnamed x1, blocking collectives  147 us
    gather x4, local copies, waits for them, and re-layouts, take_rows(): return lax.dynamic_slice_in_dim(doubled_rows, start_row, SIDE, 0)  123 us
    unnamed x9, waiting for transfers between devices  44.6 us
    unnamed x22, local copies, waits for them, and re-layouts  26.7 us
    unnamed x8, starting transfers between devices  23.4 us
    dot_general x1, matrix products, shards(): lax.dot_general(shifted, template_piece, (((1,), (1,)), ((), ())), prefer...  19.7 us
    pmax x1, blocking collectives, shards(): peak_value = lax.pmax(local_peak, ('cls', 'own'))  15.3 us
    psum x1, blocking collectives, shards(): mass_total = lax.psum(jnp.sum(exps, axis=1), ('cls', 'own'))  13.7 us
  transfers between devices with their start and end apart: 9, of which 5 were waited for; matrix products, arithmetic and copies ran while one was open for 30% of the time, Pallas kernels for 0%

commit v1 on v0

v1 whole, which is shorter than its diff:
```python
import functools

import jax
import jax.numpy as jnp
from jax import lax
from jax.experimental import pallas as pl
from jax.experimental.pallas import tpu as pltpu
from jax.sharding import Mesh, PartitionSpec as P

SIDE = 64
ORIENT_PER_BLOCK = 64
BLOCK_PRIOR_GAIN = 1.5
XS = 4
ZS = 8
LEAD = 8
LAST = 4
VMEM = 56 * 1024 * 1024


def shift_kernel(off_ref, img_ref, out_ref):
    image = img_ref[...]
    turned = jnp.concatenate([image[:, SIDE:], image[:, :SIDE]], axis=1)
    offsets = off_ref[...]

    def pick(amount, bit, yes, no):
        flag = ((amount >> bit) & 1).astype(jnp.float32).astype(jnp.bfloat16)
        return jnp.where(jnp.broadcast_to(flag, image.shape) > 0, yes, no)

    for s in range(out_ref.shape[0]):
        amount = offsets[:, s : s + 1]
        cur = pick(amount, 0, turned, image)
        for bit in range(1, 6):
            lanes = SIDE << bit
            rolled = jnp.concatenate([cur[:, lanes:], cur[:, :lanes]], axis=1)
            cur = pick(amount, bit, rolled, cur)
        out_ref[s] = cur


def make_shifted(images, offsets):
    count, pixels = images.shape
    shifts = offsets.shape[1]
    tile = 32
    return pl.pallas_call(
        shift_kernel,
        out_shape=jax.ShapeDtypeStruct((shifts, count, pixels), jnp.bfloat16),
        grid=(count // tile,),
        in_specs=[
            pl.BlockSpec((tile, shifts), lambda i: (i, 0)),
            pl.BlockSpec((tile, pixels), lambda i: (i, 0)),
        ],
        out_specs=pl.BlockSpec((shifts, tile, pixels), lambda i: (0, i, 0)),
        compiler_params=pltpu.CompilerParams(vmem_limit_bytes=VMEM),
        cost_estimate=pl.CostEstimate(
            flops=20 * count * pixels * shifts, bytes_accessed=2 * count * pixels * (1 + shifts), transcendentals=0
        ),
        name="shift",
    )(offsets, images)


def score_kernel(*refs, starts):
    count = len(starts)
    bias_ref, noise_ref, prior_ref, block_ref, img_ref = refs[:5]
    piece_refs = refs[5 : 5 + count]
    exps_ref, stat_ref, table_ref, energy_ref = refs[5 + count :]
    shifts, tile, pixels = img_ref.shape

    @pl.when(pl.program_id(0) == 0)
    def _():
        for start, piece in zip(starts, piece_refs):
            table_ref[start : start + piece.shape[0], :] = piece[...]
        total = jnp.zeros((table_ref.shape[0], 128), jnp.float32)
        for c in range(0, pixels, 128):
            part = table_ref[:, c : c + 128].astype(jnp.float32)
            total = total + part * part
        energy_ref[...] = 0.5 * jnp.sum(total, axis=1, keepdims=True)

    noise = noise_ref[...]
    gain = jnp.where(block_ref[...] == prior_ref[...], BLOCK_PRIOR_GAIN, 0.0) + bias_ref[0]
    half_energy = energy_ref[...]
    table = table_ref[...]
    peak = None
    for s in range(0, shifts, 2):
        pair = img_ref[s : s + 2].reshape(2 * tile, pixels)
        corr = lax.dot_general(table, pair, (((1,), (1,)), ((), ())), preferred_element_type=jnp.float32)
        for j in range(2):
            score = noise * (corr[:, j * tile : (j + 1) * tile] - half_energy) + gain
            exps_ref[s + j] = score
            top = jnp.max(score, axis=0, keepdims=True)
            peak = top if peak is None else jnp.maximum(peak, top)
    total = jnp.zeros_like(peak)
    for s in range(shifts):
        exps = jnp.exp(exps_ref[s] - peak)
        exps_ref[s] = exps
        total = total + jnp.sum(exps, axis=0, keepdims=True)
    stat_ref[0:1, :] = peak
    stat_ref[1:2, :] = total


def scores(bias, noise, prior, block, table_pieces, shifted):
    shifts, count, pixels = shifted.shape
    starts, orient = [], 0
    for piece in table_pieces:
        starts.append(orient)
        orient += piece.shape[0]
    tile = 128
    return pl.pallas_call(
        functools.partial(score_kernel, starts=tuple(starts)),
        out_shape=(
            jax.ShapeDtypeStruct((shifts, orient, count), jnp.float32),
            jax.ShapeDtypeStruct((2, count), jnp.float32),
        ),
        grid=(count // tile,),
        in_specs=[
            pl.BlockSpec(memory_space=pltpu.SMEM),
            pl.BlockSpec((1, tile), lambda i: (0, i)),
            pl.BlockSpec((1, tile), lambda i: (0, i)),
            pl.BlockSpec((orient, 1), lambda i: (0, 0)),
            pl.BlockSpec((shifts, tile, pixels), lambda i: (0, i, 0)),
        ]
        + [pl.BlockSpec(piece.shape, lambda i: (0, 0)) for piece in table_pieces],
        out_specs=(
            pl.BlockSpec((shifts, orient, tile), lambda i: (0, 0, i)),
            pl.BlockSpec((2, tile), lambda i: (0, i)),
        ),
        scratch_shapes=[pltpu.VMEM((orient, pixels), jnp.bfloat16), pltpu.VMEM((orient, 1), jnp.float32)],
        compiler_params=pltpu.CompilerParams(vmem_limit_bytes=VMEM),
        cost_estimate=pl.CostEstimate(
            flops=2 * shifts * count * pixels * orient,
            bytes_accessed=2 * shifts * count * pixels + 2 * orient * pixels + 4 * shifts * count * orient,
            transcendentals=shifts * count * orient,
        ),
        name="scores",
    )(bias, noise, prior, block, shifted, *table_pieces)


def project_kernel(*refs, others, keep):
    stat_refs = refs[: others + 1]
    exps_ref, img_ref = refs[others + 1 : others + 3]
    out_refs = refs[others + 3 : -2]
    post_ref, weight_ref = refs[-2:]
    shifts, count, width = img_ref.shape

    @pl.when(pl.program_id(0) == 0)
    def _():
        peak = stat_refs[0][0:1, :]
        for ref in stat_refs[1:]:
            peak = jnp.maximum(peak, ref[0:1, :])
        parts = [ref[1:2, :] * jnp.exp(ref[0:1, :] - peak) for ref in stat_refs]
        mass = parts[0]
        for part in parts[1:]:
            mass = mass + part
        post_ref[...] = (parts[0] + parts[1]) / mass
        factor = jnp.exp(stat_refs[0][0:1, :] - peak) / mass
        for s in range(shifts):
            exps = jnp.concatenate([exps_ref[s, start:stop, :] for start, stop in keep], axis=0)
            weight_ref[:, s * count : (s + 1) * count] = (exps * factor).astype(jnp.bfloat16)

    image = img_ref[...].reshape(shifts * count, width)
    sums = jnp.dot(weight_ref[...], image, preferred_element_type=jnp.float32)
    row = 0
    for ref in out_refs:
        ref[...] = sums[row : row + ref.shape[0]].astype(ref.dtype)
        row += ref.shape[0]


def project(stats, exps, shifted, keep, outs):
    shifts, count, pixels = shifted.shape
    orient = exps.shape[1]
    width = 512
    return pl.pallas_call(
        functools.partial(project_kernel, others=len(stats) - 1, keep=tuple(keep)),
        out_shape=tuple(jax.ShapeDtypeStruct((size, pixels), kind) for size, kind in outs)
        + (jax.ShapeDtypeStruct((1, count), jnp.float32),),
        grid=(pixels // width,),
        in_specs=[pl.BlockSpec(stat.shape, lambda i: (0, 0)) for stat in stats]
        + [
            pl.BlockSpec(exps.shape, lambda i: (0, 0, 0)),
            pl.BlockSpec((shifts, count, width), lambda i: (0, 0, i)),
        ],
        out_specs=tuple(pl.BlockSpec((size, width), lambda i: (0, i)) for size, _ in outs)
        + (pl.BlockSpec((1, count), lambda i: (0, 0)),),
        scratch_shapes=[pltpu.VMEM((orient, shifts * count), jnp.bfloat16)],
        compiler_params=pltpu.CompilerParams(vmem_limit_bytes=VMEM),
        cost_estimate=pl.CostEstimate(
            flops=2 * shifts * count * pixels * orient,
            bytes_accessed=2 * shifts * count * pixels + 4 * orient * pixels + 4 * shifts * count * orient,
            transcendentals=0,
        ),
        name="project",
    )(*stats, exps, shifted)


def hop(axis, size, by):
    return axis, [(i, (i + by) % size) for i in range(size)]


def exchange(messages, together=()):
    held = lax.optimization_barrier(tuple(value for value, _ in messages) + tuple(together))
    sent = tuple(lax.ppermute(value, route[0], route[1]) for value, (_, route) in zip(held, messages))
    return lax.optimization_barrier(sent)


def orient_index(per_device):
    x, own = lax.axis_index("x"), lax.axis_index("c")
    dx = jnp.arange(XS, dtype=jnp.int32)
    z = jnp.arange(ZS, dtype=jnp.int32)
    owner = z[:, None] + ((x - dx) % XS)[None, :] * ZS
    row = owner[:, :, None] * (2 * per_device) + own * per_device + jnp.arange(per_device, dtype=jnp.int32)
    lead = row[:, :, :LEAD].transpose(1, 0, 2)
    return jnp.concatenate([lead.reshape(-1), row[:, :, LEAD:].reshape(-1)])


def share_stats(stats):
    messages = []
    for dy, dc in [(0, 1), (1, 0), (3, 0), (1, 1), (3, 1), (2, 0), (2, 1)]:
        pairs = [(y * 2 + c, (y + dy) % 4 * 2 + (c + dc) % 2) for y in range(4) for c in range(2)]
        messages.append((stats, (("y", "c"), pairs)))
    return (stats,) + exchange(messages)


def row_plan(per_device):
    follow = per_device - LEAD
    start = XS * ZS * LEAD

    def lead(z, dx):
        first = (dx * ZS + z) * LEAD
        return (first, first + LEAD)

    def rest(z, dx, low, high):
        first = start + (z * XS + dx) * follow - LEAD
        return (first + low, first + high)

    def block(dx, zs):
        plan = []
        for z in zs:
            plan += [lead(z, dx), rest(z, dx, LEAD, per_device - LAST)]
        return plan

    low, high = range(ZS // 2), range(ZS // 2, ZS)
    direct = [rest(z, dx, per_device - LAST, per_device) for z in range(ZS) for dx in range(XS)]
    plan = direct + block(2, low) + block(1, high) + block(2, high) + block(3, low)
    return plan + block(1, low) + block(3, high) + block(0, low) + block(0, high)


def gather_templates(rows, images, offsets):
    lead, follow = rows[:LEAD], rows[LEAD:]
    near = exchange([(follow, hop("x", XS, d)) for d in range(1, XS)])
    near = jnp.concatenate((follow,) + near, axis=0)
    near, lead = lax.optimization_barrier((near, lead))
    table = lax.all_gather(near, "z", axis=0, tiled=True)
    p_0 = lax.all_gather(lead, "z", axis=0, tiled=True)
    shifted = make_shifted(images, offsets)
    p_1, p_3 = exchange([(p_0, hop("x", XS, 1)), (p_0, hop("x", XS, -1))])
    cut = p_0.shape[0] // 2
    p_2 = exchange([(p_1[:cut], hop("x", XS, 1)), (p_3[cut:], hop("x", XS, -1))], (shifted,))
    return [p_0, p_1, p_2[0], p_2[1], p_3, table], shifted


def shards(images, templates, offsets, groups, prior_block, group_weight, class_log_prior):
    per_device, pixels = templates.shape[1:]
    table, shifted = gather_templates(templates[0], images, offsets)
    onehot = groups[:, None] == jnp.arange(group_weight.shape[0], dtype=jnp.int32)[None, :]
    noise = jnp.sum(jnp.where(onehot, group_weight[None, :], 0.0), axis=1)[None, :]
    bias = lax.dynamic_slice_in_dim(class_log_prior, lax.axis_index("y"), 1, 0)
    block = (orient_index(per_device) // ORIENT_PER_BLOCK)[:, None]
    exps, stats = scores(bias, noise, prior_block[None, :], block, table, shifted)
    stats = share_stats(stats)
    half, wide = jnp.bfloat16, jnp.float32
    turn = ZS * (per_device - LAST)
    cut = turn // 2
    outs = [(XS * ZS * LAST, wide), (turn, half), (turn, half), (turn, wide), (turn, wide)]
    direct, to_left, to_right, onward, own, post = project(stats, exps, shifted, row_plan(per_device), outs)
    direct = lax.psum_scatter(direct, "z", scatter_dimension=0, tiled=True)
    from_right, from_left = exchange([(to_left, hop("x", XS, -1)), (to_right, hop("x", XS, 1))])
    low = (onward[:cut] + from_right[:cut].astype(wide)).astype(half)
    high = (onward[cut:] + from_left[:cut].astype(wide)).astype(half)
    low, high = exchange([(low, hop("x", XS, -1)), (high, hop("x", XS, 1))])
    first = (own[:cut] + from_left[cut:].astype(wide) + low.astype(wide)).astype(half)
    second = (own[cut:] + from_right[cut:].astype(wide) + high.astype(wide)).astype(half)
    sums = jnp.concatenate([first, second], axis=0).reshape(ZS, -1, pixels // 4)
    sums = lax.all_to_all(sums, "z", 0, 0, tiled=True)
    sums = jnp.sum(sums.astype(wide), axis=0).reshape(-1, pixels)
    direct = direct.reshape(XS, LAST, pixels)
    arrived = exchange([(direct[d], hop("x", XS, -d)) for d in range(1, XS)])
    last = direct[0] + arrived[0] + arrived[1] + arrived[2]
    out = jnp.concatenate([sums, last], axis=0)
    return (post.reshape(-1, 1), out[None])


def solution(mesh):
    grid = Mesh(mesh.devices.reshape(XS, ZS, 4, 2), ("x", "z", "y", "c"))
    dom = ("x", "z")
    placed = (
        P(dom, None),
        P("y", ("x", "z", "c"), None),
        P(dom, None),
        P(dom),
        P(dom),
        P(),
        P(),
    )
    return jax.shard_map(
        shards,
        mesh=grid,
        in_specs=placed,
        out_specs=(P(dom, "y"), P("y", ("x", "z", "c"), None)),
        check_vma=False,
    )
```

time: 501 us -> 198 us (0.40); the launches traced: 496 us -> 198 us
  blocking collectives: 189 us -> 24.5 us
  local copies, waits for them, and re-layouts: 165 us -> 9.89 us
  Pallas kernels: 0 us -> 41.8 us
  matrix products: 32.8 us -> 0 us
  other arithmetic: 25.4 us -> 5.81 us
  waiting for transfers between devices: 44.6 us -> 61.8 us
  starting transfers between devices: 23.4 us -> 39.5 us
    unnamed x1 -> x0, blocking collectives: 147 us -> none
    gather x4 -> x0, local copies, waits for them, and re-layouts: 123 us -> none  [take_rows(): return lax.dynamic_slice_in_dim(doubled_rows, start_row, SIDE, 0)]
    unnamed x9 -> x2, waiting for transfers between devices: 44.6 us -> 0.03 us
    pallas_call x0 -> x3, Pallas kernels: none -> 41.8 us  [the longest x1 15.1 us: scores(): pl.pallas_call(functools.partial(score_kernel, starts=tuple(starts)), out...]
    ppermute x0 -> x21, waiting for transfers between devices: none -> 40.1 us  [exchange(): lax.ppermute(value, route[0], route[1])]
    ppermute x0 -> x21, starting transfers between devices: none -> 35 us  [exchange(): lax.ppermute(value, route[0], route[1])]
    dot_general x3 -> x0, matrix products: 32.8 us -> none  [the longest x1 19.7 us: shards(): lax.dot_general(shifted, template_piece, (((1,), (1,)), ((), ())), prefer...]
    psum x2 -> x0, blocking collectives: 27 us -> none  [the longest x1 13.7 us: shards(): mass_total = lax.psum(jnp.sum(exps, axis=1), ('cls', 'own'))]
  transfers between devices with their start and end apart: 9 -> 24, of which waited for: 5 -> 9; matrix products, arithmetic and copies ran while one was open for 30% -> 5% of each run, Pallas kernels for 0% -> 6%
where the time goes in v1:
time: 198 us
  waiting for transfers between devices  61.8 us (31%)
  Pallas kernels  41.8 us (21%)
  starting transfers between devices  39.5 us (20%)
  blocking collectives  24.5 us (12%)
  between operations  14.4 us (7%)
  local copies, waits for them, and re-layouts  9.89 us (5%)
  other arithmetic  5.81 us (3%)
    ppermute x21, waiting for transfers between devices, exchange(): lax.ppermute(value, route[0], route[1])  40.1 us
    ppermute x21, starting transfers between devices, exchange(): lax.ppermute(value, route[0], route[1])  35 us
    all_gather x1, blocking collectives, gather_templates(): p_0 = lax.all_gather(lead, 'z', axis=0, tiled=True)  24.5 us
    all_to_all x1, waiting for transfers between devices, shards(): sums = lax.all_to_all(sums, 'z', 0, 0, tiled=True)  21.7 us
    pallas_call x1, Pallas kernels, scores(): pl.pallas_call(functools.partial(score_kernel, starts=tuple(starts)), out...  15.1 us
    pallas_call x1, Pallas kernels, project(): pl.pallas_call(functools.partial(project_kernel, others=len(stats) - 1, k...  14.7 us
    pallas_call x1, Pallas kernels, make_shifted(): pl.pallas_call(shift_kernel, out_shape=jax.ShapeDtypeStruct((shifts, coun...  12.1 us
    all_to_all x1, starting transfers between devices, shards(): sums = lax.all_to_all(sums, 'z', 0, 0, tiled=True)  4.46 us
  transfers between devices with their start and end apart: 24, of which 9 were waited for; matrix products, arithmetic and copies ran while one was open for 5% of the time, Pallas kernels for 6%

profile of v1, /device:TPU:1, one launch (start us, length us, event | category | flops | bytes accessed | tf_op | source)
XLA Modules:
  0.0 197.7 jit_solution(533518206495527039)
XLA Ops:
  7.2 0.9 slice_bitcast_fusion
  8.1 2.1 %collective-permute-start = (bf16[10,4096]{1,0:T(8,128)(2,1)S(1)}, bf16[10,4096]{1,0:T(8,128)(2,1)S(1)}, u32[]{:S(2)}, u32[]{:S(2)}) collective-permute-start(bf16[10,4096]{1,0:T(8,128)(2,1)S(1)} %slice_bitcast_fusion), channel_id=1, source_target_pairs={{0,64},{64,128},{128,192},{192,0},{1,65},{65,129},{129,193},{193,1... | collective-permute-start | bytes 245768 | tf_op jit(solution)/shard_map/ppermute | solution.py:199
  10.3 2.5 %collective-permute-start.1 = (bf16[10,4096]{1,0:T(8,128)(2,1)S(1)}, bf16[10,4096]{1,0:T(8,128)(2,1)S(1)}, u32[]{:S(2)}, u32[]{:S(2)}) collective-permute-start(bf16[10,4096]{1,0:T(8,128)(2,1)S(1)} %slice_bitcast_fusion), channel_id=1, source_target_pairs={{0,128},{64,192},{128,0},{192,64},{1,129},{65,193},{129,1},{193,65... | collective-permute-start | bytes 245768 | tf_op jit(solution)/shard_map/ppermute | solution.py:199
  12.7 1.2 collective-permute-start.2
  13.9 0.8 slice_bitcast_fusion.1
  14.7 3.7 %collective-permute-done.1 = bf16[10,4096]{1,0:T(8,128)(2,1)S(1)} collective-permute-done((bf16[10,4096]{1,0:T(8,128)(2,1)S(1)}, bf16[10,4096]{1,0:T(8,128)(2,1)S(1)}, u32[]{:S(2)}, u32[]{:S(2)}) %collective-permute-start.1) | collective-permute-done | bytes 81952 | tf_op jit(solution)/shard_map/ppermute | solution.py:199
  18.4 0.9 pad_maximum_fusion.2
  19.4 24.5 %all_gather.6.refs_5_ = bf16[64,4096]{1,0:T(8,128)(2,1)S(1)} all-gather(bf16[8,4096]{1,0:T(8,128)(2,1)S(1)} %slice_bitcast_fusion.1), channel_id=1, replica_groups=mesh['x'=4,'z'=8,'y'=4,'c'=2] {'z'}, dimensions={0}, use_global_device_ids=true | all-gather | bytes 589824 | tf_op jit(solution)/shard_map/all_gather | solution.py:251
  43.9 1.0 collective-permute-start.3
  44.9 1.6 collective-permute-start.4
  46.9 0.8 copy.26.off_ref
  47.8 12.1 %shift.1.refs_4_.refs_9_ = bf16[4,384,4096]{2,1,0:T(8,128)(2,1)} custom-call(s32[384,4]{1,0:T(8,128)} %copy.26.off_ref, bf16[384,4096]{1,0:T(8,128)(2,1)} %img_ref.1), custom_call_target="tpu_custom_call" | custom-call | flops 125829120 | bytes 15728640 | tf_op jit(solution)/shard_map/shift/pallas_call | solution.py:43
  60.1 2.7 %collective-permute-start.6 = (bf16[32,4096]{1,0:T(8,128)(2,1)S(1)}, bf16[32,4096]{1,0:T(8,128)(2,1)S(1)}, u32[]{:S(2)}, u32[]{:S(2)}) collective-permute-start(bf16[32,4096]{1,0:T(8,128)(2,1)S(1)} %slice.71), channel_id=1, source_target_pairs={{0,192},{64,0},{128,64},{192,128},{1,193},{65,1},{129,65},{193,129... | collective-permute-start | bytes 786440 | tf_op jit(solution)/shard_map/ppermute | solution.py:199
  62.8 0.6 broadcast_in_dim.32.refs_2_
  63.4 0.6 broadcast_in_dim.31.refs_1_
  64.1 0.7 dynamic_slice.3.refs_0_
  64.7 0.9 add_select_fusion.refs_3_
  65.6 1.3 collective-permute-done.5.refs_7_
  67.0 0.6 copy-done.9
  67.8 15.1 %scores.1 = (f32[4,576,384]{2,1,0:T(8,128)}, f32[2,384]{1,0:T(2,128)}) custom-call(f32[1]{0:T(128)} %dynamic_slice.3.refs_0_, f32[1,384]{1,0:T(1,128)} %broadcast_in_dim.31.refs_1_, s32[1,384]{1,0:T(1,128)} %broadcast_in_dim.32.refs_2_, s32[576,1]{1,0:T(8,128)} %add_select_fusion.refs_3_, bf16[4,384,4096]{2,1,0:T(8,128)(2,1)} %shift.1.refs_4_.refs_9_, ...), custom_call_target="tpu_custom_call" | custom-call | flops 7247757312 | bytes 20840448 | tf_op jit(solution)/shard_map/scores/pallas_call | solution.py:106
  82.9 8.2 %collective-permute-start.7 = (f32[2,384]{1,0:T(2,128)}, f32[2,384]{1,0:T(2,128)S(1)}, u32[]{:S(2)}, u32[]{:S(2)}) collective-permute-start(f32[2,384]{1,0:T(2,128)} %get-tuple-element.77.refs_0_), channel_id=1, source_target_pairs={{0,1},{1,0},{2,3},{3,2},{4,5},{5,4},{6,7},{7,6},{8,9},{9,8},{10,11... | collective-permute-start | bytes 9224 | tf_op jit(solution)/shard_map/ppermute | solution.py:199
  91.1 1.4 collective-permute-start.8
  92.5 1.5 collective-permute-start.9
  94.0 0.5 collective-permute-start.10
  94.4 2.5 %collective-permute-start.11 = (f32[2,384]{1,0:T(2,128)}, f32[2,384]{1,0:T(2,128)S(1)}, u32[]{:S(2)}, u32[]{:S(2)}) collective-permute-start(f32[2,384]{1,0:T(2,128)} %get-tuple-element.77.refs_0_), channel_id=1, source_target_pairs={{0,7},{1,6},{2,1},{3,0},{4,3},{5,2},{6,5},{7,4},{8,15},{9,14},{10,... | collective-permute-start | bytes 9224 | tf_op jit(solution)/shard_map/ppermute | solution.py:199
  96.9 0.4 collective-permute-start.12
  97.3 3.4 %collective-permute-start.13 = (f32[2,384]{1,0:T(2,128)}, f32[2,384]{1,0:T(2,128)S(1)}, u32[]{:S(2)}, u32[]{:S(2)}) collective-permute-start(f32[2,384]{1,0:T(2,128)} %get-tuple-element.77.refs_0_), channel_id=1, source_target_pairs={{0,5},{1,4},{2,7},{3,6},{4,1},{5,0},{6,3},{7,2},{8,13},{9,12},{10,... | collective-permute-start | bytes 9224 | tf_op jit(solution)/shard_map/ppermute | solution.py:199
  100.7 0.3 collective-permute-done.12.refs_6_
  101.1 1.4 collective-permute-done.13.refs_7_
  102.5 0.6 copy-done.17
  103.1 14.7 %project.1 = (f32[128,4096]{1,0:T(8,128)}, bf16[112,4096]{1,0:T(8,128)(2,1)}, bf16[112,4096]{1,0:T(8,128)(2,1)}, f32[112,4096]{1,0:T(8,128)}, f32[112,4096]{1,0:T(8,128)}, /*index=5*/f32[1,384]{1,0:T(1,128)}) custom-call(f32[2,384]{1,0:T(2,128)} %get-tuple-element.77.refs_0_, f32[2,384]{1,0:T(2,128)} %copy-done.11, f32[2,384]{1,0:T(2,128)} %copy-done.12, ...), custom_call_target="tpu_custom_call" | custom-call | flops 7247757312 | bytes 25559040 | tf_op jit(solution)/shard_map/project/pallas_call | solution.py:170
  117.7 2.9 %collective-permute-start.14 = (bf16[112,4096]{1,0:T(8,128)(2,1)}, bf16[112,4096]{1,0:T(8,128)(2,1)S(1)}, u32[]{:S(2)}, u32[]{:S(2)}) collective-permute-start(bf16[112,4096]{1,0:T(8,128)(2,1)} %get-tuple-element.90), channel_id=1, source_target_pairs={{0,192},{64,0},{128,64},{192,128},{1,193},{65,1},{129,65},{193,129... | collective-permute-start | bytes 2752520 | tf_op jit(solution)/shard_map/ppermute | solution.py:199
  120.7 19.5 %collective-permute-done.14 = bf16[112,4096]{1,0:T(8,128)(2,1)S(1)} collective-permute-done((bf16[112,4096]{1,0:T(8,128)(2,1)}, bf16[112,4096]{1,0:T(8,128)(2,1)S(1)}, u32[]{:S(2)}, u32[]{:S(2)}) %collective-permute-start.14) | collective-permute-done | bytes 917536 | tf_op jit(solution)/shard_map/ppermute | solution.py:199
  140.2 3.1 %collective-permute-done.15 = bf16[112,4096]{1,0:T(8,128)(2,1)} collective-permute-done((bf16[112,4096]{1,0:T(8,128)(2,1)}, bf16[112,4096]{1,0:T(8,128)(2,1)}, u32[]{:S(2)}, u32[]{:S(2)}) %collective-permute-start.15) | collective-permute-done | bytes 917536 | tf_op jit(solution)/shard_map/ppermute | solution.py:199
  143.3 1.3 add_convert_fusion.2
  144.7 0.4 collective-permute-start.16
  145.1 1.1 collective-permute-start.17
  146.2 9.0 %collective-permute-done.16 = bf16[56,4096]{1,0:T(8,128)(2,1)S(1)} collective-permute-done((bf16[56,4096]{1,0:T(8,128)(2,1)S(1)}, bf16[56,4096]{1,0:T(8,128)(2,1)S(1)}, u32[]{:S(2)}, u32[]{:S(2)}) %collective-permute-start.16) | collective-permute-done | bytes 458784 | tf_op jit(solution)/shard_map/ppermute | solution.py:199
  155.2 1.7 collective-permute-done.17
  156.9 1.3 add_convert_fusion.1
  158.3 1.5 reshape.214
  159.8 4.5 %all-to-all-start = ((bf16[8,56,1024]{2,1,0:T(8,128)(2,1)}), bf16[8,56,1024]{2,1,0:T(8,128)(2,1)S(1)}, u32[]{:S(2)}, u32[]{:S(2)}) async-start(bf16[8,56,1024]{2,1,0:T(8,128)(2,1)} %reshape.214), calls=%async_computation | async-start | bytes 1835008 | tf_op jit(solution)/shard_map/all_to_all | solution.py:281
  164.3 1.1 fusion.6
  165.3 0.2 collective-permute-start.18
  165.6 1.1 collective-permute-start.19
  166.9 21.7 %all-to-all-done = bf16[8,56,1024]{2,1,0:T(8,128)(2,1)S(1)} async-done(((bf16[8,56,1024]{2,1,0:T(8,128)(2,1)}), bf16[8,56,1024]{2,1,0:T(8,128)(2,1)S(1)}, u32[]{:S(2)}, u32[]{:S(2)}) %all-to-all-start) | async-done | bytes 917536 | tf_op jit(solution)/shard_map/all_to_all | solution.py:281
  188.8 0.9 fusion.3
  189.8 1.0 broadcast_in_dim.33
  (75 shorter events, 1.6 us)
Async XLA Ops:
  7.2 39.8 %copy-start.5 = (s32[384,4]{0,1:T(4,128)S(1)}, s32[384,4]{0,1:T(4,128)}, u32[]{:S(2)}) copy-start(s32[384,4]{0,1:T(4,128)} %param.9) | copy-start | bytes 18436
  7.2 59.8 %all-gather.2.cloned.1.call-start = ((), (), s32[]{:S(2)}) async-start(), calls=%async_computation.2 | async-start | bytes 2949120 | tf_op jit(solution)/shard_map/all_gather | solution.py:250
  8.1 6.6 %collective-permute-start = (bf16[10,4096]{1,0:T(8,128)(2,1)S(1)}, bf16[10,4096]{1,0:T(8,128)(2,1)S(1)}, u32[]{:S(2)}, u32[]{:S(2)}) collective-permute-start(bf16[10,4096]{1,0:T(8,128)(2,1)S(1)} %slice_bitcast_fusion), channel_id=1, source_target_pairs={{0,64},{64,128},{128,192},{192,0},{1,65},{65,129},{129,193},{193,1... | collective-permute-start | bytes 245768 | tf_op jit(solution)/shard_map/ppermute | solution.py:199
  10.3 8.2 %collective-permute-start.1 = (bf16[10,4096]{1,0:T(8,128)(2,1)S(1)}, bf16[10,4096]{1,0:T(8,128)(2,1)S(1)}, u32[]{:S(2)}, u32[]{:S(2)}) collective-permute-start(bf16[10,4096]{1,0:T(8,128)(2,1)S(1)} %slice_bitcast_fusion), channel_id=1, source_target_pairs={{0,128},{64,192},{128,0},{192,64},{1,129},{65,193},{129,1},{193,65... | collective-permute-start | bytes 245768 | tf_op jit(solution)/shard_map/ppermute | solution.py:199
  12.7 5.7 %collective-permute-start.2 = (bf16[10,4096]{1,0:T(8,128)(2,1)S(1)}, bf16[10,4096]{1,0:T(8,128)(2,1)S(1)}, u32[]{:S(2)}, u32[]{:S(2)}) collective-permute-start(bf16[10,4096]{1,0:T(8,128)(2,1)S(1)} %slice_bitcast_fusion), channel_id=1, source_target_pairs={{0,192},{64,0},{128,64},{192,128},{1,193},{65,1},{129,65},{193,129... | collective-permute-start | bytes 245768 | tf_op jit(solution)/shard_map/ppermute | solution.py:199
  19.3 144.9 %reduce-scatter.2.cloned.1.call-start = ((), (), s32[]{:S(2)}) async-start(), calls=%async_computation.3 | async-start | bytes 2359296 | tf_op jit(solution)/shard_map/reduce_scatter | solution.py:273
  43.9 16.0 %copy-start.2 = (bf16[64,4096]{1,0:T(8,128)(2,1)}, bf16[64,4096]{1,0:T(8,128)(2,1)S(1)}, u32[]{:S(2)}) copy-start(bf16[64,4096]{1,0:T(8,128)(2,1)S(1)} %all_gather.6.refs_5_) | copy-start | bytes 1572868
  43.9 16.1 %collective-permute-start.3 = (bf16[64,4096]{1,0:T(8,128)(2,1)S(1)}, bf16[64,4096]{1,0:T(8,128)(2,1)S(1)}, u32[]{:S(2)}, u32[]{:S(2)}) collective-permute-start(bf16[64,4096]{1,0:T(8,128)(2,1)S(1)} %all_gather.6.refs_5_), channel_id=1, source_target_pairs={{0,64},{64,128},{128,192},{192,0},{1,65},{65,129},{129,193},{193,1... | collective-permute-start | bytes 1572872 | tf_op jit(solution)/shard_map/ppermute | solution.py:199
  44.9 15.0 %collective-permute-start.4 = (bf16[64,4096]{1,0:T(8,128)(2,1)S(1)}, bf16[64,4096]{1,0:T(8,128)(2,1)S(1)}, u32[]{:S(2)}, u32[]{:S(2)}) collective-permute-start(bf16[64,4096]{1,0:T(8,128)(2,1)S(1)} %all_gather.6.refs_5_), channel_id=1, source_target_pairs={{0,192},{64,0},{128,64},{192,128},{1,193},{65,1},{129,65},{193,129... | collective-permute-start | bytes 1572872 | tf_op jit(solution)/shard_map/ppermute | solution.py:199
  47.8 12.1 %copy-start.7 = (s32[384]{0:T(512)S(1)}, s32[384]{0:T(512)}, u32[]{:S(2)}) copy-start(s32[384]{0:T(512)} %param.10) | copy-start | bytes 4612
  47.8 12.1 %copy-start.8 = (f32[16]{0:T(128)S(1)}, f32[16]{0:T(128)}, u32[]{:S(2)}) copy-start(f32[16]{0:T(128)} %param.12) | copy-start | bytes 196
  47.8 15.0 %copy-start.6 = (s32[384]{0:T(512)S(1)}, s32[384]{0:T(512)}, u32[]{:S(2)}) copy-start(s32[384]{0:T(512)} %param.11) | copy-start | bytes 4612
  47.8 16.3 %copy-start.18 = (f32[4]{0:T(128)S(1)}, f32[4]{0:T(128)}, u32[]{:S(2)}) copy-start(f32[4]{0:T(128)} %param.13) | copy-start | bytes 52
  60.0 7.0 %copy-start.3 = (bf16[64,4096]{1,0:T(8,128)(2,1)}, bf16[64,4096]{1,0:T(8,128)(2,1)S(1)}, u32[]{:S(2)}) copy-start(bf16[64,4096]{1,0:T(8,128)(2,1)S(1)} %collective-permute-done.3.refs_6_) | copy-start | bytes 1572868
  60.0 7.0 %copy-start.4 = (bf16[64,4096]{1,0:T(8,128)(2,1)}, bf16[64,4096]{1,0:T(8,128)(2,1)S(1)}, u32[]{:S(2)}) copy-start(bf16[64,4096]{1,0:T(8,128)(2,1)S(1)} %collective-permute-done.4.refs_9_) | copy-start | bytes 1572868
  60.0 6.9 %collective-permute-start.5 = (bf16[32,4096]{1,0:T(8,128)(2,1)S(1)}, bf16[32,4096]{1,0:T(8,128)(2,1)S(1)}, u32[]{:S(2)}, u32[]{:S(2)}) collective-permute-start(bf16[32,4096]{1,0:T(8,128)(2,1)S(1)} %slice.70), channel_id=1, source_target_pairs={{0,64},{64,128},{128,192},{192,0},{1,65},{65,129},{129,193},{193,1... | collective-permute-start | bytes 786440 | tf_op jit(solution)/shard_map/ppermute | solution.py:199
  60.1 6.8 %collective-permute-start.6 = (bf16[32,4096]{1,0:T(8,128)(2,1)S(1)}, bf16[32,4096]{1,0:T(8,128)(2,1)S(1)}, u32[]{:S(2)}, u32[]{:S(2)}) collective-permute-start(bf16[32,4096]{1,0:T(8,128)(2,1)S(1)} %slice.71), channel_id=1, source_target_pairs={{0,192},{64,0},{128,64},{192,128},{1,193},{65,1},{129,65},{193,129... | collective-permute-start | bytes 786440 | tf_op jit(solution)/shard_map/ppermute | solution.py:199
  66.9 0.7 copy-start.9
  66.9 0.8 copy-start.10
  82.9 14.1 %collective-permute-start.7 = (f32[2,384]{1,0:T(2,128)}, f32[2,384]{1,0:T(2,128)S(1)}, u32[]{:S(2)}, u32[]{:S(2)}) collective-permute-start(f32[2,384]{1,0:T(2,128)} %get-tuple-element.77.refs_0_), channel_id=1, source_target_pairs={{0,1},{1,0},{2,3},{3,2},{4,5},{5,4},{6,7},{7,6},{8,9},{9,8},{10,11... | collective-permute-start | bytes 9224 | tf_op jit(solution)/shard_map/ppermute | solution.py:199
  91.1 6.2 %collective-permute-start.8 = (f32[2,384]{1,0:T(2,128)}, f32[2,384]{1,0:T(2,128)S(1)}, u32[]{:S(2)}, u32[]{:S(2)}) collective-permute-start(f32[2,384]{1,0:T(2,128)} %get-tuple-element.77.refs_0_), channel_id=1, source_target_pairs={{0,2},{1,3},{2,4},{3,5},{4,6},{5,7},{6,0},{7,1},{8,10},{9,11},{10,... | collective-permute-start | bytes 9224 | tf_op jit(solution)/shard_map/ppermute | solution.py:199
  92.5 8.2 %collective-permute-start.9 = (f32[2,384]{1,0:T(2,128)}, f32[2,384]{1,0:T(2,128)S(1)}, u32[]{:S(2)}, u32[]{:S(2)}) collective-permute-start(f32[2,384]{1,0:T(2,128)} %get-tuple-element.77.refs_0_), channel_id=1, source_target_pairs={{0,6},{1,7},{2,0},{3,1},{4,2},{5,3},{6,4},{7,5},{8,14},{9,15},{10,... | collective-permute-start | bytes 9224 | tf_op jit(solution)/shard_map/ppermute | solution.py:199
  94.0 6.7 %collective-permute-start.10 = (f32[2,384]{1,0:T(2,128)}, f32[2,384]{1,0:T(2,128)S(1)}, u32[]{:S(2)}, u32[]{:S(2)}) collective-permute-start(f32[2,384]{1,0:T(2,128)} %get-tuple-element.77.refs_0_), channel_id=1, source_target_pairs={{0,3},{1,2},{2,5},{3,4},{4,7},{5,6},{6,1},{7,0},{8,11},{9,10},{10,... | collective-permute-start | bytes 9224 | tf_op jit(solution)/shard_map/ppermute | solution.py:199
  94.4 6.3 %collective-permute-start.11 = (f32[2,384]{1,0:T(2,128)}, f32[2,384]{1,0:T(2,128)S(1)}, u32[]{:S(2)}, u32[]{:S(2)}) collective-permute-start(f32[2,384]{1,0:T(2,128)} %get-tuple-element.77.refs_0_), channel_id=1, source_target_pairs={{0,7},{1,6},{2,1},{3,0},{4,3},{5,2},{6,5},{7,4},{8,15},{9,14},{10,... | collective-permute-start | bytes 9224 | tf_op jit(solution)/shard_map/ppermute | solution.py:199
  96.9 5.6 %copy-start.11 = (f32[2,384]{1,0:T(2,128)}, f32[2,384]{1,0:T(2,128)S(1)}, u32[]{:S(2)}) copy-start(f32[2,384]{1,0:T(2,128)S(1)} %collective-permute-done.7.refs_1_) | copy-start | bytes 9220
  96.9 4.2 %collective-permute-start.12 = (f32[2,384]{1,0:T(2,128)}, f32[2,384]{1,0:T(2,128)S(1)}, u32[]{:S(2)}, u32[]{:S(2)}) collective-permute-start(f32[2,384]{1,0:T(2,128)} %get-tuple-element.77.refs_0_), channel_id=1, source_target_pairs={{0,4},{1,5},{2,6},{3,7},{4,0},{5,1},{6,2},{7,3},{8,12},{9,13},{10,... | collective-permute-start | bytes 9224 | tf_op jit(solution)/shard_map/ppermute | solution.py:199
  97.3 5.2 %copy-start.12 = (f32[2,384]{1,0:T(2,128)}, f32[2,384]{1,0:T(2,128)S(1)}, u32[]{:S(2)}) copy-start(f32[2,384]{1,0:T(2,128)S(1)} %collective-permute-done.8.refs_2_) | copy-start | bytes 9220
  97.3 5.2 %collective-permute-start.13 = (f32[2,384]{1,0:T(2,128)}, f32[2,384]{1,0:T(2,128)S(1)}, u32[]{:S(2)}, u32[]{:S(2)}) collective-permute-start(f32[2,384]{1,0:T(2,128)} %get-tuple-element.77.refs_0_), channel_id=1, source_target_pairs={{0,5},{1,4},{2,7},{3,6},{4,1},{5,0},{6,3},{7,2},{8,13},{9,12},{10,... | collective-permute-start | bytes 9224 | tf_op jit(solution)/shard_map/ppermute | solution.py:199
  100.7 1.8 copy-start.13
  100.7 1.8 copy-start.14
  100.7 1.8 copy-start.15
  101.1 1.4 copy-start.16
  102.5 0.6 copy-start.17
  117.7 25.6 %copy-start.1 = (f32[112,4096]{1,0:T(8,128)S(1)}, f32[112,4096]{1,0:T(8,128)}, u32[]{:S(2)}) copy-start(f32[112,4096]{1,0:T(8,128)} %get-tuple-element.93) | copy-start | bytes 5505028
  117.7 22.5 %collective-permute-start.14 = (bf16[112,4096]{1,0:T(8,128)(2,1)}, bf16[112,4096]{1,0:T(8,128)(2,1)S(1)}, u32[]{:S(2)}, u32[]{:S(2)}) collective-permute-start(bf16[112,4096]{1,0:T(8,128)(2,1)} %get-tuple-element.90), channel_id=1, source_target_pairs={{0,192},{64,0},{128,64},{192,128},{1,193},{65,1},{129,65},{193,129... | collective-permute-start | bytes 2752520 | tf_op jit(solution)/shard_map/ppermute | solution.py:199
  120.7 22.6 %collective-permute-start.15 = (bf16[112,4096]{1,0:T(8,128)(2,1)}, bf16[112,4096]{1,0:T(8,128)(2,1)}, u32[]{:S(2)}, u32[]{:S(2)}) collective-permute-start(bf16[112,4096]{1,0:T(8,128)(2,1)} %get-tuple-element.91), channel_id=1, source_target_pairs={{0,64},{64,128},{128,192},{192,0},{1,65},{65,129},{129,193},{193,1... | collective-permute-start | bytes 2752520 | tf_op jit(solution)/shard_map/ppermute | solution.py:199
  143.3 13.6 %copy-start = (f32[112,4096]{1,0:T(8,128)S(1)}, f32[112,4096]{1,0:T(8,128)}, u32[]{:S(2)}) copy-start(f32[112,4096]{1,0:T(8,128)} %get-tuple-element.87) | copy-start | bytes 5505028
  144.7 10.5 %collective-permute-start.16 = (bf16[56,4096]{1,0:T(8,128)(2,1)S(1)}, bf16[56,4096]{1,0:T(8,128)(2,1)S(1)}, u32[]{:S(2)}, u32[]{:S(2)}) collective-permute-start(bf16[56,4096]{1,0:T(8,128)(2,1)S(1)} %get-tuple-element.95), channel_id=1, source_target_pairs={{0,192},{64,0},{128,64},{192,128},{1,193},{65,1},{129,65},{193,129... | collective-permute-start | bytes 1376264 | tf_op jit(solution)/shard_map/ppermute | solution.py:199
  145.1 11.8 %collective-permute-start.17 = (bf16[56,4096]{1,0:T(8,128)(2,1)S(1)}, bf16[56,4096]{1,0:T(8,128)(2,1)S(1)}, u32[]{:S(2)}, u32[]{:S(2)}) collective-permute-start(bf16[56,4096]{1,0:T(8,128)(2,1)S(1)} %get-tuple-element.96), channel_id=1, source_target_pairs={{0,64},{64,128},{128,192},{192,0},{1,65},{65,129},{129,193},{193,1... | collective-permute-start | bytes 1376264 | tf_op jit(solution)/shard_map/ppermute | solution.py:199
  159.8 28.7 %all-to-all-start = ((bf16[8,56,1024]{2,1,0:T(8,128)(2,1)}), bf16[8,56,1024]{2,1,0:T(8,128)(2,1)S(1)}, u32[]{:S(2)}, u32[]{:S(2)}) async-start(bf16[8,56,1024]{2,1,0:T(8,128)(2,1)} %reshape.214), calls=%async_computation | async-start | bytes 1835008 | tf_op jit(solution)/shard_map/all_to_all | solution.py:281
  165.3 23.5 %collective-permute-start.18 = (f32[4,4096]{1,0:T(4,128)S(1)}, f32[4,4096]{1,0:T(4,128)S(1)}, u32[]{:S(2)}, u32[]{:S(2)}) collective-permute-start(f32[4,4096]{1,0:T(4,128)S(1)} %get-tuple-element.100), channel_id=1, source_target_pairs={{0,192},{64,0},{128,64},{192,128},{1,193},{65,1},{129,65},{193,129... | collective-permute-start | bytes 196616 | tf_op jit(solution)/shard_map/ppermute | solution.py:199
  165.6 23.2 %collective-permute-start.19 = (f32[4,4096]{1,0:T(4,128)S(1)}, f32[4,4096]{1,0:T(4,128)S(1)}, u32[]{:S(2)}, u32[]{:S(2)}) collective-permute-start(f32[4,4096]{1,0:T(4,128)S(1)} %get-tuple-element.101), channel_id=1, source_target_pairs={{0,128},{64,192},{128,0},{192,64},{1,129},{65,193},{129,1},{193,65... | collective-permute-start | bytes 196616 | tf_op jit(solution)/shard_map/ppermute | solution.py:199
  166.7 22.1 %collective-permute-start.20 = (f32[4,4096]{1,0:T(4,128)S(1)}, f32[4,4096]{1,0:T(4,128)S(1)}, u32[]{:S(2)}, u32[]{:S(2)}) collective-permute-start(f32[4,4096]{1,0:T(4,128)S(1)} %get-tuple-element.102), channel_id=1, source_target_pairs={{0,64},{64,128},{128,192},{192,0},{1,65},{65,129},{129,193},{193,1... | collective-permute-start | bytes 196616 | tf_op jit(solution)/shard_map/ppermute | solution.py:199
Sparse Core Ops, SparseCore 0:
  19.5 45.6 all-gather.1
  120.8 37.2 reduce-scatter.1

commit v2 on v1

--- a/solution.py
+++ b/solution.py
@@ -13,7 +13,7 @@
 XS = 4
 ZS = 8
 LEAD = 8
-LAST = 4
+LAST = 6
 VMEM = 56 * 1024 * 1024
 
 
@@ -133,24 +133,21 @@
     )(bias, noise, prior, block, shifted, *table_pieces)
 
 
-def project_kernel(*refs, others, keep):
-    stat_refs = refs[: others + 1]
-    exps_ref, img_ref = refs[others + 1 : others + 3]
-    out_refs = refs[others + 3 : -2]
+def project_kernel(*refs, keep):
+    cls_ref, all_ref, own_ref, exps_ref, img_ref = refs[:5]
+    out_refs = refs[5:-2]
     post_ref, weight_ref = refs[-2:]
     shifts, count, width = img_ref.shape
 
     @pl.when(pl.program_id(0) == 0)
     def _():
-        peak = stat_refs[0][0:1, :]
-        for ref in stat_refs[1:]:
-            peak = jnp.maximum(peak, ref[0:1, :])
-        parts = [ref[1:2, :] * jnp.exp(ref[0:1, :] - peak) for ref in stat_refs]
-        mass = parts[0]
-        for part in parts[1:]:
-            mass = mass + part
-        post_ref[...] = (parts[0] + parts[1]) / mass
-        factor = jnp.exp(stat_refs[0][0:1, :] - peak) / mass
+        peaks = all_ref[:, 0, :]
+        peak = jnp.max(peaks, axis=0, keepdims=True)
+        parts = all_ref[:, 1, :] * jnp.exp(peaks - peak)
+        mass = jnp.sum(parts, axis=0, keepdims=True)
+        member = lax.broadcasted_iota(jnp.int32, parts.shape, 0) // 2 == cls_ref[0]
+        post_ref[...] = jnp.sum(jnp.where(member, parts, 0.0), axis=0, keepdims=True) / mass
+        factor = jnp.exp(own_ref[0:1, :] - peak) / mass
         for s in range(shifts):
             exps = jnp.concatenate([exps_ref[s, start:stop, :] for start, stop in keep], axis=0)
             weight_ref[:, s * count : (s + 1) * count] = (exps * factor).astype(jnp.bfloat16)
@@ -163,17 +160,19 @@
         row += ref.shape[0]
 
 
-def project(stats, exps, shifted, keep, outs):
+def project(cls_index, gathered, own, exps, shifted, keep, outs):
     shifts, count, pixels = shifted.shape
     orient = exps.shape[1]
     width = 512
     return pl.pallas_call(
-        functools.partial(project_kernel, others=len(stats) - 1, keep=tuple(keep)),
+        functools.partial(project_kernel, keep=tuple(keep)),
         out_shape=tuple(jax.ShapeDtypeStruct((size, pixels), kind) for size, kind in outs)
         + (jax.ShapeDtypeStruct((1, count), jnp.float32),),
         grid=(pixels // width,),
-        in_specs=[pl.BlockSpec(stat.shape, lambda i: (0, 0)) for stat in stats]
-        + [
+        in_specs=[
+            pl.BlockSpec(memory_space=pltpu.SMEM),
+            pl.BlockSpec(gathered.shape, lambda i: (0, 0, 0)),
+            pl.BlockSpec(own.shape, lambda i: (0, 0)),
             pl.BlockSpec(exps.shape, lambda i: (0, 0, 0)),
             pl.BlockSpec((shifts, count, width), lambda i: (0, 0, i)),
         ],
@@ -187,7 +186,7 @@
             transcendentals=0,
         ),
         name="project",
-    )(*stats, exps, shifted)
+    )(cls_index, gathered, own, exps, shifted)
 
 
 def hop(axis, size, by):
@@ -210,14 +209,6 @@
     return jnp.concatenate([lead.reshape(-1), row[:, :, LEAD:].reshape(-1)])
 
 
-def share_stats(stats):
-    messages = []
-    for dy, dc in [(0, 1), (1, 0), (3, 0), (1, 1), (3, 1), (2, 0), (2, 1)]:
-        pairs = [(y * 2 + c, (y + dy) % 4 * 2 + (c + dc) % 2) for y in range(4) for c in range(2)]
-        messages.append((stats, (("y", "c"), pairs)))
-    return (stats,) + exchange(messages)
-
-
 def row_plan(per_device):
     follow = per_device - LEAD
     start = XS * ZS * LEAD
@@ -233,7 +224,9 @@
     def block(dx, zs):
         plan = []
         for z in zs:
-            plan += [lead(z, dx), rest(z, dx, LEAD, per_device - LAST)]
+            plan.append(lead(z, dx))
+            if LEAD < per_device - LAST:
+                plan.append(rest(z, dx, LEAD, per_device - LAST))
         return plan
 
     low, high = range(ZS // 2), range(ZS // 2, ZS)
@@ -245,10 +238,10 @@
 def gather_templates(rows, images, offsets):
     lead, follow = rows[:LEAD], rows[LEAD:]
     near = exchange([(follow, hop("x", XS, d)) for d in range(1, XS)])
+    p_0 = lax.all_to_all(jnp.tile(lead, (ZS, 1)), "z", 0, 0, tiled=True)
     near = jnp.concatenate((follow,) + near, axis=0)
-    near, lead = lax.optimization_barrier((near, lead))
+    near, p_0 = lax.optimization_barrier((near, p_0))
     table = lax.all_gather(near, "z", axis=0, tiled=True)
-    p_0 = lax.all_gather(lead, "z", axis=0, tiled=True)
     shifted = make_shifted(images, offsets)
     p_1, p_3 = exchange([(p_0, hop("x", XS, 1)), (p_0, hop("x", XS, -1))])
     cut = p_0.shape[0] // 2
@@ -261,15 +254,18 @@
     table, shifted = gather_templates(templates[0], images, offsets)
     onehot = groups[:, None] == jnp.arange(group_weight.shape[0], dtype=jnp.int32)[None, :]
     noise = jnp.sum(jnp.where(onehot, group_weight[None, :], 0.0), axis=1)[None, :]
-    bias = lax.dynamic_slice_in_dim(class_log_prior, lax.axis_index("y"), 1, 0)
+    cls_index = lax.axis_index("y")
+    bias = lax.dynamic_slice_in_dim(class_log_prior, cls_index, 1, 0)
     block = (orient_index(per_device) // ORIENT_PER_BLOCK)[:, None]
     exps, stats = scores(bias, noise, prior_block[None, :], block, table, shifted)
-    stats = share_stats(stats)
+    gathered = lax.all_to_all(jnp.broadcast_to(stats[None], (8,) + stats.shape), ("y", "c"), 0, 0, tiled=True)
     half, wide = jnp.bfloat16, jnp.float32
     turn = ZS * (per_device - LAST)
     cut = turn // 2
     outs = [(XS * ZS * LAST, wide), (turn, half), (turn, half), (turn, wide), (turn, wide)]
-    direct, to_left, to_right, onward, own, post = project(stats, exps, shifted, row_plan(per_device), outs)
+    direct, to_left, to_right, onward, own, post = project(
+        cls_index[None], gathered, stats, exps, shifted, row_plan(per_device), outs
+    )
     direct = lax.psum_scatter(direct, "z", scatter_dimension=0, tiled=True)
     from_right, from_left = exchange([(to_left, hop("x", XS, -1)), (to_right, hop("x", XS, 1))])
     low = (onward[:cut] + from_right[:cut].astype(wide)).astype(half)

time: 198 us -> 186 us (0.939)
  blocking collectives: 24.5 us -> 12.6 us
  waiting for transfers between devices: 61.8 us -> 70.7 us
  starting transfers between devices: 39.5 us -> 31.2 us
  other arithmetic: 5.81 us -> 3.54 us
    all_gather x1 -> x0, blocking collectives: 24.5 us -> none  [gather_templates(): p_0 = lax.all_gather(lead, 'z', axis=0, tiled=True)]
    ppermute x21 -> x14, starting transfers between devices: 35 us -> 18.2 us  [exchange(): lax.ppermute(value, route[0], route[1])]
    all_to_all x0 -> x1, blocking collectives: none -> 12.6 us  [shards(): lax.all_to_all(jnp.broadcast_to(stats[None], (8,) + stats.shape), ('y', '...]
    all_gather x1, waiting for transfers between devices: 0.02 us -> 11.2 us  [gather_templates(): table = lax.all_gather(near, 'z', axis=0, tiled=True)]
    all_to_all x0 -> x1, starting transfers between devices: none -> 9.01 us  [gather_templates(): p_0 = lax.all_to_all(jnp.tile(lead, (ZS, 1)), 'z', 0, 0, tiled=True)]
    all_to_all x0 -> x1, waiting for transfers between devices: none -> 7.72 us  [gather_templates(): p_0 = lax.all_to_all(jnp.tile(lead, (ZS, 1)), 'z', 0, 0, tiled=True)]
    all_to_all x1, waiting for transfers between devices: 21.7 us -> 14.7 us  [shards(): sums = lax.all_to_all(sums, 'z', 0, 0, tiled=True)]
    ppermute x21 -> x14, waiting for transfers between devices: 40.1 us -> 35.3 us  [exchange(): lax.ppermute(value, route[0], route[1])]
  transfers between devices with their start and end apart: 24 -> 18, of which waited for: 9 -> 12; matrix products, arithmetic and copies ran while one was open for 5% -> 4% of each run, Pallas kernels for 6% -> 7%
where the time goes in v2:
time: 186 us; the launch traced here: 184 us
  waiting for transfers between devices  70.7 us (38%)
  Pallas kernels  41.9 us (23%)
  starting transfers between devices  31.2 us (17%)
  between operations  14.3 us (8%)
  blocking collectives  12.6 us (7%)
  local copies, waits for them, and re-layouts  10.2 us (5%)
  other arithmetic  3.54 us (2%)
    ppermute x14, waiting for transfers between devices, exchange(): lax.ppermute(value, route[0], route[1])  35.3 us
    ppermute x14, starting transfers between devices, exchange(): lax.ppermute(value, route[0], route[1])  18.2 us
    pallas_call x1, Pallas kernels, scores(): pl.pallas_call(functools.partial(score_kernel, starts=tuple(starts)), out...  15.1 us
    pallas_call x1, Pallas kernels, project(): pl.pallas_call(functools.partial(project_kernel, keep=tuple(keep)), out_s...  14.7 us
    all_to_all x1, waiting for transfers between devices, shards(): sums = lax.all_to_all(sums, 'z', 0, 0, tiled=True)  14.7 us
    all_to_all x1, blocking collectives, shards(): lax.all_to_all(jnp.broadcast_to(stats[None], (8,) + stats.shape), ('y', '...  12.6 us
    pallas_call x1, Pallas kernels, make_shifted(): pl.pallas_call(shift_kernel, out_shape=jax.ShapeDtypeStruct((shifts, coun...  12 us
    all_gather x1, waiting for transfers between devices, gather_templates(): table = lax.all_gather(near, 'z', axis=0, tiled=True)  11.2 us
  transfers between devices with their start and end apart: 18, of which 12 were waited for; matrix products, arithmetic and copies ran while one was open for 4% of the time, Pallas kernels for 7%

profile of v2, /device:TPU:1, one launch (start us, length us, event | category | flops | bytes accessed | tf_op | source)
XLA Modules:
  0.0 184.4 jit_solution(39651086643867568)
XLA Ops:
  7.2 0.9 slice_bitcast_fusion.1
  8.1 0.8 tile.10
  8.9 9.0 %all-to-all-start = ((bf16[8,8,4096]{2,1,0:T(8,128)(2,1)}), bf16[8,8,4096]{2,1,0:T(8,128)(2,1)S(1)}, u32[]{:S(2)}, u32[]{:S(2)}) async-start(bf16[8,8,4096]{2,1,0:T(8,128)(2,1)} %tile.10), calls=%async_computation | async-start | bytes 1048576 | tf_op jit(solution)/shard_map/all_to_all | solution.py:241
  18.0 1.3 collective-permute-start
  19.3 2.5 %collective-permute-start.1 = (bf16[10,4096]{1,0:T(8,128)(2,1)S(1)}, bf16[10,4096]{1,0:T(8,128)(2,1)S(1)}, u32[]{:S(2)}, u32[]{:S(2)}) collective-permute-start(bf16[10,4096]{1,0:T(8,128)(2,1)S(1)} %slice_bitcast_fusion), channel_id=1, source_target_pairs={{0,128},{64,192},{128,0},{192,64},{1,129},{65,193},{129,1},{193,65... | collective-permute-start | bytes 245768 | tf_op jit(solution)/shard_map/ppermute | solution.py:198
  21.7 1.2 collective-permute-start.2
  22.9 0.2 collective-permute-done
  23.1 4.0 %collective-permute-done.1 = bf16[10,4096]{1,0:T(8,128)(2,1)S(1)} collective-permute-done((bf16[10,4096]{1,0:T(8,128)(2,1)S(1)}, bf16[10,4096]{1,0:T(8,128)(2,1)S(1)}, u32[]{:S(2)}, u32[]{:S(2)}) %collective-permute-start.1) | collective-permute-done | bytes 81952 | tf_op jit(solution)/shard_map/ppermute | solution.py:198
  27.1 0.1 collective-permute-done.2
  27.2 0.9 pad_maximum_fusion.2
  28.2 7.7 %all-to-all-done = bf16[8,8,4096]{2,1,0:T(8,128)(2,1)S(1)} async-done(((bf16[8,8,4096]{2,1,0:T(8,128)(2,1)}), bf16[8,8,4096]{2,1,0:T(8,128)(2,1)S(1)}, u32[]{:S(2)}, u32[]{:S(2)}) %all-to-all-start) | async-done | bytes 524320 | tf_op jit(solution)/shard_map/all_to_all | solution.py:241
  36.0 1.3 collective-permute-start.3
  37.3 1.5 collective-permute-start.4
  38.9 0.1 concatenate.42
  39.1 0.8 copy.26.off_ref
  40.0 12.0 %shift.1.refs_4_ = bf16[4,384,4096]{2,1,0:T(8,128)(2,1)} custom-call(s32[384,4]{1,0:T(8,128)} %copy.26.off_ref, bf16[384,4096]{1,0:T(8,128)(2,1)} %img_ref.1), custom_call_target="tpu_custom_call" | custom-call | flops 125829120 | bytes 15728640 | tf_op jit(solution)/shard_map/shift/pallas_call | solution.py:43
  52.3 2.7 %collective-permute-start.6 = (bf16[32,4096]{1,0:T(8,128)(2,1)S(1)}, bf16[32,4096]{1,0:T(8,128)(2,1)S(1)}, u32[]{:S(2)}, u32[]{:S(2)}) collective-permute-start(bf16[32,4096]{1,0:T(8,128)(2,1)S(1)} %slice.68), channel_id=1, source_target_pairs={{0,192},{64,0},{128,64},{192,128},{1,193},{65,1},{129,65},{193,129... | collective-permute-start | bytes 786440 | tf_op jit(solution)/shard_map/ppermute | solution.py:198
  54.9 0.6 broadcast_in_dim.42.refs_2_
  55.5 0.6 broadcast_in_dim.41.refs_1_
  56.1 0.2 copy.22
  56.2 0.7 dynamic_slice.3.refs_0_
  56.9 0.9 add_select_fusion.refs_3_
  57.8 2.6 %collective-permute-done.5.refs_7_ = bf16[32,4096]{1,0:T(8,128)(2,1)S(1)} collective-permute-done((bf16[32,4096]{1,0:T(8,128)(2,1)S(1)}, bf16[32,4096]{1,0:T(8,128)(2,1)S(1)}, u32[]{:S(2)}, u32[]{:S(2)}) %collective-permute-start.5) | collective-permute-done | bytes 262176 | tf_op jit(solution)/shard_map/ppermute | solution.py:198
  60.3 11.2 %all-gather.2.cloned.1.call-done.refs_10_ = bf16[320,4096]{1,0:T(8,128)(2,1)} async-done(((bf16[40,4096]{1,0:T(8,128)(2,1)}), bf16[320,4096]{1,0:T(8,128)(2,1)}) %all-gather.2.cloned.1.call-update) | async-done | bytes 2621456 | tf_op jit(solution)/shard_map/all_gather | solution.py:244
  71.6 15.1 %scores.1 = (f32[4,576,384]{2,1,0:T(8,128)}, f32[2,384]{1,0:T(2,128)}) custom-call(f32[1]{0:T(128)} %dynamic_slice.3.refs_0_, f32[1,384]{1,0:T(1,128)} %broadcast_in_dim.41.refs_1_, s32[1,384]{1,0:T(1,128)} %broadcast_in_dim.42.refs_2_, s32[576,1]{1,0:T(8,128)} %add_select_fusion.refs_3_, bf16[4,384,4096]{2,1,0:T(8,128)(2,1)} %shift.1.refs_4_, ...), custom_call_target="tpu_custom_call" | custom-call | flops 7247757312 | bytes 20840448 | tf_op jit(solution)/shard_map/scores/pallas_call | solution.py:106
  86.7 0.7 broadcast_in_dim.43
  87.4 12.6 %all_to_all.19.refs_1_ = f32[8,2,384]{2,1,0:T(2,128)} all-to-all(f32[8,2,384]{2,1,0:T(2,128)S(1)} %broadcast_in_dim.43), channel_id=1, replica_groups=mesh['x'=4,'z'=8,'y'=4,'c'=2] {'y','c'}, dimensions={0} | all-to-all | bytes 49152 | tf_op jit(solution)/shard_map/all_to_all | solution.py:261
  100.0 14.7 %project.1 = (f32[192,4096]{1,0:T(8,128)}, bf16[96,4096]{1,0:T(8,128)(2,1)}, bf16[96,4096]{1,0:T(8,128)(2,1)}, f32[96,4096]{1,0:T(8,128)}, f32[96,4096]{1,0:T(8,128)}, /*index=5*/f32[1,384]{1,0:T(1,128)}) custom-call(s32[1]{0:T(128)} %bitcast.refs_0_, f32[8,2,384]{2,1,0:T(2,128)} %all_to_all.19.refs_1_, f32[2,384]{1,0:T(2,128)} %get-tuple-element.56.refs_2_, ...), custom_call_target="tpu_custom_call" | custom-call | flops 7247757312 | bytes 25559040 | tf_op jit(solution)/shard_map/project/pallas_call | solution.py:167
  114.7 1.1 copy-done.11
  115.8 2.6 %collective-permute-start.7 = (bf16[96,4096]{1,0:T(8,128)(2,1)S(1)}, bf16[96,4096]{1,0:T(8,128)(2,1)S(1)}, u32[]{:S(2)}, u32[]{:S(2)}) collective-permute-start(bf16[96,4096]{1,0:T(8,128)(2,1)S(1)} %copy-done.11), channel_id=1, source_target_pairs={{0,192},{64,0},{128,64},{192,128},{1,193},{65,1},{129,65},{193,129... | collective-permute-start | bytes 2359304 | tf_op jit(solution)/shard_map/ppermute | solution.py:198
  118.5 16.1 %collective-permute-done.7 = bf16[96,4096]{1,0:T(8,128)(2,1)S(1)} collective-permute-done((bf16[96,4096]{1,0:T(8,128)(2,1)S(1)}, bf16[96,4096]{1,0:T(8,128)(2,1)S(1)}, u32[]{:S(2)}, u32[]{:S(2)}) %collective-permute-start.7) | collective-permute-done | bytes 786464 | tf_op jit(solution)/shard_map/ppermute | solution.py:198
  134.6 3.2 %collective-permute-done.8 = bf16[96,4096]{1,0:T(8,128)(2,1)S(1)} collective-permute-done((bf16[96,4096]{1,0:T(8,128)(2,1)S(1)}, bf16[96,4096]{1,0:T(8,128)(2,1)S(1)}, u32[]{:S(2)}, u32[]{:S(2)}) %collective-permute-start.8) | collective-permute-done | bytes 786464 | tf_op jit(solution)/shard_map/ppermute | solution.py:198
  137.8 0.2 add_convert_fusion.2
  138.0 0.4 collective-permute-start.9
  138.4 1.1 collective-permute-start.10
  139.6 7.4 %collective-permute-done.9 = bf16[48,4096]{1,0:T(8,128)(2,1)S(1)} collective-permute-done((bf16[48,4096]{1,0:T(8,128)(2,1)S(1)}, bf16[48,4096]{1,0:T(8,128)(2,1)S(1)}, u32[]{:S(2)}, u32[]{:S(2)}) %collective-permute-start.9) | collective-permute-done | bytes 393248 | tf_op jit(solution)/shard_map/ppermute | solution.py:198
  147.0 1.6 collective-permute-done.10
  148.6 0.2 add_convert_fusion.1
  148.9 1.4 reshape.223
  150.2 3.9 %all-to-all-start.2 = ((bf16[8,48,1024]{2,1,0:T(8,128)(2,1)}), bf16[8,48,1024]{2,1,0:T(8,128)(2,1)S(1)}, u32[]{:S(2)}, u32[]{:S(2)}) async-start(bf16[8,48,1024]{2,1,0:T(8,128)(2,1)} %reshape.223), calls=%async_computation.2 | async-start | bytes 1572864 | tf_op jit(solution)/shard_map/all_to_all | solution.py:277
  154.1 1.8 reduce-scatter.2.cloned.1.call-done
  155.9 1.1 fusion.6
  157.0 2.7 %collective-permute-start.11 = (f32[6,4096]{1,0:T(8,128)S(1)}, f32[6,4096]{1,0:T(8,128)S(1)}, u32[]{:S(2)}, u32[]{:S(2)}) collective-permute-start(f32[6,4096]{1,0:T(8,128)S(1)} %get-tuple-element.72), channel_id=1, source_target_pairs={{0,192},{64,0},{128,64},{192,128},{1,193},{65,1},{129,65},{193,129... | collective-permute-start | bytes 294920 | tf_op jit(solution)/shard_map/ppermute | solution.py:198
  159.7 0.5 collective-permute-start.12
  160.2 0.4 collective-permute-start.13
  160.6 14.7 %all-to-all-done.2 = bf16[8,48,1024]{2,1,0:T(8,128)(2,1)S(1)} async-done(((bf16[8,48,1024]{2,1,0:T(8,128)(2,1)}), bf16[8,48,1024]{2,1,0:T(8,128)(2,1)S(1)}, u32[]{:S(2)}, u32[]{:S(2)}) %all-to-all-start.2) | async-done | bytes 786464 | tf_op jit(solution)/shard_map/all_to_all | solution.py:277
  175.6 0.9 fusion.3
  176.6 1.0 broadcast_in_dim.44
  (57 shorter events, 1.0 us)
Async XLA Ops:
  7.2 10.8 %copy-start.3 = (bf16[1,18,4096]{2,1,0:T(8,128)(2,1)S(1)}, bf16[1,18,4096]{2,1,0:T(8,128)(2,1)}, u32[]{:S(2)}) copy-start(bf16[1,18,4096]{2,1,0:T(8,128)(2,1)} %param.8) | copy-start | bytes 442372
  8.1 31.0 %copy-start.6 = (s32[384,4]{0,1:T(4,128)S(1)}, s32[384,4]{0,1:T(4,128)}, u32[]{:S(2)}) copy-start(s32[384,4]{0,1:T(4,128)} %param.9) | copy-start | bytes 18436
  8.9 27.0 %all-to-all-start = ((bf16[8,8,4096]{2,1,0:T(8,128)(2,1)}), bf16[8,8,4096]{2,1,0:T(8,128)(2,1)S(1)}, u32[]{:S(2)}, u32[]{:S(2)}) async-start(bf16[8,8,4096]{2,1,0:T(8,128)(2,1)} %tile.10), calls=%async_computation | async-start | bytes 1048576 | tf_op jit(solution)/shard_map/all_to_all | solution.py:241
  17.9 53.6 %all-gather.2.cloned.1.call-start = ((), (), s32[]{:S(2)}) async-start(), calls=%async_computation.4 | async-start | bytes 2949120 | tf_op jit(solution)/shard_map/all_gather | solution.py:244
  18.0 5.1 %collective-permute-start = (bf16[10,4096]{1,0:T(8,128)(2,1)S(1)}, bf16[10,4096]{1,0:T(8,128)(2,1)S(1)}, u32[]{:S(2)}, u32[]{:S(2)}) collective-permute-start(bf16[10,4096]{1,0:T(8,128)(2,1)S(1)} %slice_bitcast_fusion), channel_id=1, source_target_pairs={{0,64},{64,128},{128,192},{192,0},{1,65},{65,129},{129,193},{193,1... | collective-permute-start | bytes 245768 | tf_op jit(solution)/shard_map/ppermute | solution.py:198
  19.3 7.8 %collective-permute-start.1 = (bf16[10,4096]{1,0:T(8,128)(2,1)S(1)}, bf16[10,4096]{1,0:T(8,128)(2,1)S(1)}, u32[]{:S(2)}, u32[]{:S(2)}) collective-permute-start(bf16[10,4096]{1,0:T(8,128)(2,1)S(1)} %slice_bitcast_fusion), channel_id=1, source_target_pairs={{0,128},{64,192},{128,0},{192,64},{1,129},{65,193},{129,1},{193,65... | collective-permute-start | bytes 245768 | tf_op jit(solution)/shard_map/ppermute | solution.py:198
  21.7 5.5 %collective-permute-start.2 = (bf16[10,4096]{1,0:T(8,128)(2,1)S(1)}, bf16[10,4096]{1,0:T(8,128)(2,1)S(1)}, u32[]{:S(2)}, u32[]{:S(2)}) collective-permute-start(bf16[10,4096]{1,0:T(8,128)(2,1)S(1)} %slice_bitcast_fusion), channel_id=1, source_target_pairs={{0,192},{64,0},{128,64},{192,128},{1,193},{65,1},{129,65},{193,129... | collective-permute-start | bytes 245768 | tf_op jit(solution)/shard_map/ppermute | solution.py:198
  35.9 16.1 %copy-start.2 = (bf16[8,8,4096]{2,1,0:T(8,128)(2,1)}, bf16[8,8,4096]{2,1,0:T(8,128)(2,1)S(1)}, u32[]{:S(2)}) copy-start(bf16[8,8,4096]{2,1,0:T(8,128)(2,1)S(1)} %all-to-all-done) | copy-start | bytes 1572868
  35.9 120.0 %reduce-scatter.2.cloned.1.call-start = ((), (), s32[]{:S(2)}) async-start(), calls=%async_computation.5 | async-start | bytes 3538944 | tf_op jit(solution)/shard_map/reduce_scatter | solution.py:269
  36.0 16.1 %collective-permute-start.3 = (bf16[64,4096]{1,0:T(8,128)(2,1)S(1)}, bf16[64,4096]{1,0:T(8,128)(2,1)S(1)}, u32[]{:S(2)}, u32[]{:S(2)}) collective-permute-start(bf16[64,4096]{1,0:T(8,128)(2,1)S(1)} %bitcast.9), channel_id=1, source_target_pairs={{0,64},{64,128},{128,192},{192,0},{1,65},{65,129},{129,193},{193,1... | collective-permute-start | bytes 1572872 | tf_op jit(solution)/shard_map/ppermute | solution.py:198
  37.3 14.8 %collective-permute-start.4 = (bf16[64,4096]{1,0:T(8,128)(2,1)S(1)}, bf16[64,4096]{1,0:T(8,128)(2,1)S(1)}, u32[]{:S(2)}, u32[]{:S(2)}) collective-permute-start(bf16[64,4096]{1,0:T(8,128)(2,1)S(1)} %bitcast.10), channel_id=1, source_target_pairs={{0,192},{64,0},{128,64},{192,128},{1,193},{65,1},{129,65},{193,129... | collective-permute-start | bytes 1572872 | tf_op jit(solution)/shard_map/ppermute | solution.py:198
  40.0 12.0 %copy-start.8 = (s32[384]{0:T(512)S(1)}, s32[384]{0:T(512)}, u32[]{:S(2)}) copy-start(s32[384]{0:T(512)} %param.10) | copy-start | bytes 4612
  40.0 12.0 %copy-start.9 = (f32[16]{0:T(128)S(1)}, f32[16]{0:T(128)}, u32[]{:S(2)}) copy-start(f32[16]{0:T(128)} %param.12) | copy-start | bytes 196
  40.0 15.0 %copy-start.7 = (s32[384]{0:T(512)S(1)}, s32[384]{0:T(512)}, u32[]{:S(2)}) copy-start(s32[384]{0:T(512)} %param.11) | copy-start | bytes 4612
  40.0 16.3 %copy-start.14 = (f32[4]{0:T(128)S(1)}, f32[4]{0:T(128)}, u32[]{:S(2)}) copy-start(f32[4]{0:T(128)} %param.13) | copy-start | bytes 52
  52.1 19.4 %copy-start.4 = (bf16[64,4096]{1,0:T(8,128)(2,1)}, bf16[64,4096]{1,0:T(8,128)(2,1)S(1)}, u32[]{:S(2)}) copy-start(bf16[64,4096]{1,0:T(8,128)(2,1)S(1)} %collective-permute-done.3.refs_6_) | copy-start | bytes 1572868
  52.1 19.4 %copy-start.5 = (bf16[64,4096]{1,0:T(8,128)(2,1)}, bf16[64,4096]{1,0:T(8,128)(2,1)S(1)}, u32[]{:S(2)}) copy-start(bf16[64,4096]{1,0:T(8,128)(2,1)S(1)} %collective-permute-done.4.refs_9_) | copy-start | bytes 1572868
  52.2 8.2 %collective-permute-start.5 = (bf16[32,4096]{1,0:T(8,128)(2,1)S(1)}, bf16[32,4096]{1,0:T(8,128)(2,1)S(1)}, u32[]{:S(2)}, u32[]{:S(2)}) collective-permute-start(bf16[32,4096]{1,0:T(8,128)(2,1)S(1)} %slice.67), channel_id=1, source_target_pairs={{0,64},{64,128},{128,192},{192,0},{1,65},{65,129},{129,193},{193,1... | collective-permute-start | bytes 786440 | tf_op jit(solution)/shard_map/ppermute | solution.py:198
  52.3 8.1 %collective-permute-start.6 = (bf16[32,4096]{1,0:T(8,128)(2,1)S(1)}, bf16[32,4096]{1,0:T(8,128)(2,1)S(1)}, u32[]{:S(2)}, u32[]{:S(2)}) collective-permute-start(bf16[32,4096]{1,0:T(8,128)(2,1)S(1)} %slice.68), channel_id=1, source_target_pairs={{0,192},{64,0},{128,64},{192,128},{1,193},{65,1},{129,65},{193,129... | collective-permute-start | bytes 786440 | tf_op jit(solution)/shard_map/ppermute | solution.py:198
  60.3 11.2 %copy-start.12 = (bf16[32,4096]{1,0:T(8,128)(2,1)}, bf16[32,4096]{1,0:T(8,128)(2,1)S(1)}, u32[]{:S(2)}) copy-start(bf16[32,4096]{1,0:T(8,128)(2,1)S(1)} %collective-permute-done.5.refs_7_) | copy-start | bytes 786436
  60.3 11.2 %copy-start.13 = (bf16[32,4096]{1,0:T(8,128)(2,1)}, bf16[32,4096]{1,0:T(8,128)(2,1)S(1)}, u32[]{:S(2)}) copy-start(bf16[32,4096]{1,0:T(8,128)(2,1)S(1)} %collective-permute-done.6.refs_8_) | copy-start | bytes 786436
  114.7 1.1 copy-start.11
  114.7 3.8 %copy-start.10 = (bf16[96,4096]{1,0:T(8,128)(2,1)S(1)}, bf16[96,4096]{1,0:T(8,128)(2,1)}, u32[]{:S(2)}) copy-start(bf16[96,4096]{1,0:T(8,128)(2,1)} %get-tuple-element.63) | copy-start | bytes 2359300
  114.7 23.1 %copy-start = (f32[96,4096]{1,0:T(8,128)S(1)}, f32[96,4096]{1,0:T(8,128)}, u32[]{:S(2)}) copy-start(f32[96,4096]{1,0:T(8,128)} %get-tuple-element.65) | copy-start | bytes 4718596
  115.8 18.8 %collective-permute-start.7 = (bf16[96,4096]{1,0:T(8,128)(2,1)S(1)}, bf16[96,4096]{1,0:T(8,128)(2,1)S(1)}, u32[]{:S(2)}, u32[]{:S(2)}) collective-permute-start(bf16[96,4096]{1,0:T(8,128)(2,1)S(1)} %copy-done.11), channel_id=1, source_target_pairs={{0,192},{64,0},{128,64},{192,128},{1,193},{65,1},{129,65},{193,129... | collective-permute-start | bytes 2359304 | tf_op jit(solution)/shard_map/ppermute | solution.py:198
  118.5 19.4 %collective-permute-start.8 = (bf16[96,4096]{1,0:T(8,128)(2,1)S(1)}, bf16[96,4096]{1,0:T(8,128)(2,1)S(1)}, u32[]{:S(2)}, u32[]{:S(2)}) collective-permute-start(bf16[96,4096]{1,0:T(8,128)(2,1)S(1)} %copy-done.10), channel_id=1, source_target_pairs={{0,64},{64,128},{128,192},{192,0},{1,65},{65,129},{129,193},{193,1... | collective-permute-start | bytes 2359304 | tf_op jit(solution)/shard_map/ppermute | solution.py:198
  137.8 10.8 %copy-start.1 = (f32[96,4096]{1,0:T(8,128)S(1)}, f32[96,4096]{1,0:T(8,128)}, u32[]{:S(2)}) copy-start(f32[96,4096]{1,0:T(8,128)} %get-tuple-element.59) | copy-start | bytes 4718596
  138.0 9.0 %collective-permute-start.9 = (bf16[48,4096]{1,0:T(8,128)(2,1)S(1)}, bf16[48,4096]{1,0:T(8,128)(2,1)S(1)}, u32[]{:S(2)}, u32[]{:S(2)}) collective-permute-start(bf16[48,4096]{1,0:T(8,128)(2,1)S(1)} %get-tuple-element.67), channel_id=1, source_target_pairs={{0,192},{64,0},{128,64},{192,128},{1,193},{65,1},{129,65},{193,129... | collective-permute-start | bytes 1179656 | tf_op jit(solution)/shard_map/ppermute | solution.py:198
  138.4 10.1 %collective-permute-start.10 = (bf16[48,4096]{1,0:T(8,128)(2,1)S(1)}, bf16[48,4096]{1,0:T(8,128)(2,1)S(1)}, u32[]{:S(2)}, u32[]{:S(2)}) collective-permute-start(bf16[48,4096]{1,0:T(8,128)(2,1)S(1)} %get-tuple-element.68), channel_id=1, source_target_pairs={{0,64},{64,128},{128,192},{192,0},{1,65},{65,129},{129,193},{193,1... | collective-permute-start | bytes 1179656 | tf_op jit(solution)/shard_map/ppermute | solution.py:198
  150.2 25.1 %all-to-all-start.2 = ((bf16[8,48,1024]{2,1,0:T(8,128)(2,1)}), bf16[8,48,1024]{2,1,0:T(8,128)(2,1)S(1)}, u32[]{:S(2)}, u32[]{:S(2)}) async-start(bf16[8,48,1024]{2,1,0:T(8,128)(2,1)} %reshape.223), calls=%async_computation.2 | async-start | bytes 1572864 | tf_op jit(solution)/shard_map/all_to_all | solution.py:277
  157.0 18.5 %collective-permute-start.11 = (f32[6,4096]{1,0:T(8,128)S(1)}, f32[6,4096]{1,0:T(8,128)S(1)}, u32[]{:S(2)}, u32[]{:S(2)}) collective-permute-start(f32[6,4096]{1,0:T(8,128)S(1)} %get-tuple-element.72), channel_id=1, source_target_pairs={{0,192},{64,0},{128,64},{192,128},{1,193},{65,1},{129,65},{193,129... | collective-permute-start | bytes 294920 | tf_op jit(solution)/shard_map/ppermute | solution.py:198
  159.7 15.9 %collective-permute-start.12 = (f32[6,4096]{1,0:T(8,128)S(1)}, f32[6,4096]{1,0:T(8,128)S(1)}, u32[]{:S(2)}, u32[]{:S(2)}) collective-permute-start(f32[6,4096]{1,0:T(8,128)S(1)} %get-tuple-element.73), channel_id=1, source_target_pairs={{0,128},{64,192},{128,0},{192,64},{1,129},{65,193},{129,1},{193,65... | collective-permute-start | bytes 294920 | tf_op jit(solution)/shard_map/ppermute | solution.py:198
  160.2 15.4 %collective-permute-start.13 = (f32[6,4096]{1,0:T(8,128)S(1)}, f32[6,4096]{1,0:T(8,128)S(1)}, u32[]{:S(2)}, u32[]{:S(2)}) collective-permute-start(f32[6,4096]{1,0:T(8,128)S(1)} %get-tuple-element.74), channel_id=1, source_target_pairs={{0,64},{64,128},{128,192},{192,0},{1,65},{65,129},{129,193},{193,1... | collective-permute-start | bytes 294920 | tf_op jit(solution)/shard_map/ppermute | solution.py:198
Sparse Core Ops, SparseCore 0:
  36.0 35.4 all-gather.1
  114.8 40.9 reduce-scatter.1

commit v3 on v2

--- a/solution.py
+++ b/solution.py
@@ -57,11 +57,12 @@
     )(offsets, images)
 
 
-def score_kernel(*refs, starts):
+def score_kernel(*refs, starts, follows):
     count = len(starts)
+    before_ref = refs[5 + count] if follows else None
     bias_ref, noise_ref, prior_ref, block_ref, img_ref = refs[:5]
     piece_refs = refs[5 : 5 + count]
-    exps_ref, stat_ref, table_ref, energy_ref = refs[5 + count :]
+    exps_ref, stat_ref, table_ref, energy_ref = refs[-4:]
     shifts, tile, pixels = img_ref.shape
 
     @pl.when(pl.program_id(0) == 0)
@@ -88,6 +89,9 @@
             top = jnp.max(score, axis=0, keepdims=True)
             peak = top if peak is None else jnp.maximum(peak, top)
     total = jnp.zeros_like(peak)
+    if follows:
+        peak = jnp.maximum(peak, before_ref[0:1, :])
+        total = before_ref[1:2, :] * jnp.exp(before_ref[0:1, :] - peak)
     for s in range(shifts):
         exps = jnp.exp(exps_ref[s] - peak)
         exps_ref[s] = exps
@@ -96,7 +100,7 @@
     stat_ref[1:2, :] = total
 
 
-def scores(bias, noise, prior, block, table_pieces, shifted):
+def scores(bias, noise, prior, block, table_pieces, shifted, name, before=()):
     shifts, count, pixels = shifted.shape
     starts, orient = [], 0
     for piece in table_pieces:
@@ -104,7 +108,7 @@
         orient += piece.shape[0]
     tile = 128
     return pl.pallas_call(
-        functools.partial(score_kernel, starts=tuple(starts)),
+        functools.partial(score_kernel, starts=tuple(starts), follows=len(before) > 0),
         out_shape=(
             jax.ShapeDtypeStruct((shifts, orient, count), jnp.float32),
             jax.ShapeDtypeStruct((2, count), jnp.float32),
@@ -117,7 +121,8 @@
             pl.BlockSpec((orient, 1), lambda i: (0, 0)),
             pl.BlockSpec((shifts, tile, pixels), lambda i: (0, i, 0)),
         ]
-        + [pl.BlockSpec(piece.shape, lambda i: (0, 0)) for piece in table_pieces],
+        + [pl.BlockSpec(piece.shape, lambda i: (0, 0)) for piece in table_pieces]
+        + [pl.BlockSpec((2, tile), lambda i: (0, i)) for _ in before],
         out_specs=(
             pl.BlockSpec((shifts, orient, tile), lambda i: (0, 0, i)),
             pl.BlockSpec((2, tile), lambda i: (0, i)),
@@ -129,13 +134,14 @@
             bytes_accessed=2 * shifts * count * pixels + 2 * orient * pixels + 4 * shifts * count * orient,
             transcendentals=shifts * count * orient,
         ),
-        name="scores",
-    )(bias, noise, prior, block, shifted, *table_pieces)
+        name=name,
+    )(bias, noise, prior, block, shifted, *table_pieces, *before)
 
 
 def project_kernel(*refs, keep):
-    cls_ref, all_ref, own_ref, exps_ref, img_ref = refs[:5]
-    out_refs = refs[5:-2]
+    cls_ref, all_ref, lead_ref, own_ref, lead_exps_ref, exps_ref, img_ref = refs[:7]
+    out_refs = refs[7:-2]
+    rows_lead = lead_exps_ref.shape[1]
     post_ref, weight_ref = refs[-2:]
     shifts, count, width = img_ref.shape
 
@@ -147,10 +153,19 @@
         mass = jnp.sum(parts, axis=0, keepdims=True)
         member = lax.broadcasted_iota(jnp.int32, parts.shape, 0) // 2 == cls_ref[0]
         post_ref[...] = jnp.sum(jnp.where(member, parts, 0.0), axis=0, keepdims=True) / mass
+        lead_factor = jnp.exp(lead_ref[0:1, :] - peak) / mass
         factor = jnp.exp(own_ref[0:1, :] - peak) / mass
         for s in range(shifts):
-            exps = jnp.concatenate([exps_ref[s, start:stop, :] for start, stop in keep], axis=0)
-            weight_ref[:, s * count : (s + 1) * count] = (exps * factor).astype(jnp.bfloat16)
+            lead = lead_exps_ref[s] * lead_factor
+            rest = exps_ref[s] * factor
+            picked = []
+            for start, stop in keep:
+                if stop <= rows_lead:
+                    picked.append(lead[start:stop])
+                else:
+                    picked.append(rest[start - rows_lead : stop - rows_lead])
+            weight = jnp.concatenate(picked, axis=0)
+            weight_ref[:, s * count : (s + 1) * count] = weight.astype(jnp.bfloat16)
 
     image = img_ref[...].reshape(shifts * count, width)
     sums = jnp.dot(weight_ref[...], image, preferred_element_type=jnp.float32)
@@ -160,10 +175,10 @@
         row += ref.shape[0]
 
 
-def project(cls_index, gathered, own, exps, shifted, keep, outs):
+def project(cls_index, gathered, lead, own, lead_exps, exps, shifted, keep, outs):
     shifts, count, pixels = shifted.shape
-    orient = exps.shape[1]
-    width = 512
+    orient = lead_exps.shape[1] + exps.shape[1]
+    width = 1024
     return pl.pallas_call(
         functools.partial(project_kernel, keep=tuple(keep)),
         out_shape=tuple(jax.ShapeDtypeStruct((size, pixels), kind) for size, kind in outs)
@@ -172,7 +187,9 @@
         in_specs=[
             pl.BlockSpec(memory_space=pltpu.SMEM),
             pl.BlockSpec(gathered.shape, lambda i: (0, 0, 0)),
+            pl.BlockSpec(lead.shape, lambda i: (0, 0)),
             pl.BlockSpec(own.shape, lambda i: (0, 0)),
+            pl.BlockSpec(lead_exps.shape, lambda i: (0, 0, 0)),
             pl.BlockSpec(exps.shape, lambda i: (0, 0, 0)),
             pl.BlockSpec((shifts, count, width), lambda i: (0, 0, i)),
         ],
@@ -186,7 +203,7 @@
             transcendentals=0,
         ),
         name="project",
-    )(cls_index, gathered, own, exps, shifted)
+    )(cls_index, gathered, lead, own, lead_exps, exps, shifted)
 
 
 def hop(axis, size, by):
@@ -257,14 +274,17 @@
     cls_index = lax.axis_index("y")
     bias = lax.dynamic_slice_in_dim(class_log_prior, cls_index, 1, 0)
     block = (orient_index(per_device) // ORIENT_PER_BLOCK)[:, None]
-    exps, stats = scores(bias, noise, prior_block[None, :], block, table, shifted)
+    rows_lead = XS * ZS * LEAD
+    prior = prior_block[None, :]
+    lead_exps, lead = scores(bias, noise, prior, block[:rows_lead], table[:-1], shifted, "scores_lead")
+    exps, stats = scores(bias, noise, prior, block[rows_lead:], table[-1:], shifted, "scores_rest", (lead,))
     gathered = lax.all_to_all(jnp.broadcast_to(stats[None], (8,) + stats.shape), ("y", "c"), 0, 0, tiled=True)
     half, wide = jnp.bfloat16, jnp.float32
     turn = ZS * (per_device - LAST)
     cut = turn // 2
     outs = [(XS * ZS * LAST, wide), (turn, half), (turn, half), (turn, wide), (turn, wide)]
     direct, to_left, to_right, onward, own, post = project(
-        cls_index[None], gathered, stats, exps, shifted, row_plan(per_device), outs
+        cls_index[None], gathered, lead, stats, lead_exps, exps, shifted, row_plan(per_device), outs
     )
     direct = lax.psum_scatter(direct, "z", scatter_dimension=0, tiled=True)
     from_right, from_left = exchange([(to_left, hop("x", XS, -1)), (to_right, hop("x", XS, 1))])

time: 186 us -> 181 us (0.973)
  waiting for transfers between devices: 70.7 us -> 58.9 us
  Pallas kernels: 41.9 us -> 46.9 us
  local copies, waits for them, and re-layouts: 10.2 us -> 13.1 us
    all_gather x1, waiting for transfers between devices: 11.2 us -> 0.01 us  [gather_templates(): table = lax.all_gather(near, 'z', axis=0, tiled=True)]
    pallas_call x1 -> x2, Pallas kernels: 15.1 us -> 21.4 us  [scores(): pl.pallas_call(functools.partial(score_kernel, starts=tuple(starts), foll...]
  transfers between devices with their start and end apart: 18 -> 18, of which waited for: 12 -> 11; matrix products, arithmetic and copies ran while one was open for 4% -> 5% of each run, Pallas kernels for 7% -> 12%
where the time goes in v3:
time: 181 us; the launch traced here: 179 us
  waiting for transfers between devices  58.9 us (33%)
  Pallas kernels  46.9 us (26%)
  starting transfers between devices  31 us (17%)
  between operations  14.3 us (8%)
  local copies, waits for them, and re-layouts  13.1 us (7%)
  blocking collectives  12.1 us (7%)
  other arithmetic  2.64 us (1%)
    ppermute x14, waiting for transfers between devices, exchange(): lax.ppermute(value, route[0], route[1])  34.5 us
    pallas_call x2, Pallas kernels, scores(): pl.pallas_call(functools.partial(score_kernel, starts=tuple(starts), foll...  21.4 us
    ppermute x14, starting transfers between devices, exchange(): lax.ppermute(value, route[0], route[1])  17.9 us
    all_to_all x1, waiting for transfers between devices, shards(): sums = lax.all_to_all(sums, 'z', 0, 0, tiled=True)  14.5 us
    pallas_call x1, Pallas kernels, project(): pl.pallas_call(functools.partial(project_kernel, keep=tuple(keep)), out_s...  13.4 us
    all_to_all x1, blocking collectives, shards(): lax.all_to_all(jnp.broadcast_to(stats[None], (8,) + stats.shape), ('y', '...  12.1 us
    pallas_call x1, Pallas kernels, make_shifted(): pl.pallas_call(shift_kernel, out_shape=jax.ShapeDtypeStruct((shifts, coun...  12 us
    all_to_all x1, starting transfers between devices, gather_templates(): p_0 = lax.all_to_all(jnp.tile(lead, (ZS, 1)), 'z', 0, 0, tiled=True)  9.01 us
  transfers between devices with their start and end apart: 18, of which 11 were waited for; matrix products, arithmetic and copies ran while one was open for 5% of the time, Pallas kernels for 12%

profile of v3, /device:TPU:1, one launch (start us, length us, event | category | flops | bytes accessed | tf_op | source)
XLA Modules:
  0.0 178.9 jit_solution(2572368039905833506)
XLA Ops:
  7.2 0.9 slice_bitcast_fusion.1
  8.1 0.8 tile.10
  8.9 9.0 %all-to-all-start = ((bf16[8,8,4096]{2,1,0:T(8,128)(2,1)}), bf16[8,8,4096]{2,1,0:T(8,128)(2,1)S(1)}, u32[]{:S(2)}, u32[]{:S(2)}) async-start(bf16[8,8,4096]{2,1,0:T(8,128)(2,1)} %tile.10), calls=%async_computation | async-start | bytes 1048576 | tf_op jit(solution)/shard_map/all_to_all | solution.py:258
  18.0 1.3 collective-permute-start
  19.3 2.5 %collective-permute-start.1 = (bf16[10,4096]{1,0:T(8,128)(2,1)S(1)}, bf16[10,4096]{1,0:T(8,128)(2,1)S(1)}, u32[]{:S(2)}, u32[]{:S(2)}) collective-permute-start(bf16[10,4096]{1,0:T(8,128)(2,1)S(1)} %slice_bitcast_fusion), channel_id=1, source_target_pairs={{0,128},{64,192},{128,0},{192,64},{1,129},{65,193},{129,1},{193,65... | collective-permute-start | bytes 245768 | tf_op jit(solution)/shard_map/ppermute | solution.py:215
  21.7 1.2 collective-permute-start.2
  22.9 0.2 collective-permute-done
  23.1 4.0 %collective-permute-done.1 = bf16[10,4096]{1,0:T(8,128)(2,1)S(1)} collective-permute-done((bf16[10,4096]{1,0:T(8,128)(2,1)S(1)}, bf16[10,4096]{1,0:T(8,128)(2,1)S(1)}, u32[]{:S(2)}, u32[]{:S(2)}) %collective-permute-start.1) | collective-permute-done | bytes 81952 | tf_op jit(solution)/shard_map/ppermute | solution.py:215
  27.3 0.9 pad_maximum_fusion.2
  28.1 7.8 %all-to-all-done = bf16[8,8,4096]{2,1,0:T(8,128)(2,1)S(1)} async-done(((bf16[8,8,4096]{2,1,0:T(8,128)(2,1)}), bf16[8,8,4096]{2,1,0:T(8,128)(2,1)S(1)}, u32[]{:S(2)}, u32[]{:S(2)}) %all-to-all-start) | async-done | bytes 524320 | tf_op jit(solution)/shard_map/all_to_all | solution.py:258
  36.0 1.3 collective-permute-start.3
  37.3 1.5 collective-permute-start.4
  39.1 0.8 copy.18.off_ref
  40.0 12.0 %shift.1.refs_4_.refs_6_ = bf16[4,384,4096]{2,1,0:T(8,128)(2,1)} custom-call(s32[384,4]{1,0:T(8,128)} %copy.18.off_ref, bf16[384,4096]{1,0:T(8,128)(2,1)} %img_ref.1), custom_call_target="tpu_custom_call" | custom-call | flops 125829120 | bytes 15728640 | tf_op jit(solution)/shard_map/shift/pallas_call | solution.py:43
  52.2 2.7 %collective-permute-start.6 = (bf16[32,4096]{1,0:T(8,128)(2,1)S(1)}, bf16[32,4096]{1,0:T(8,128)(2,1)S(1)}, u32[]{:S(2)}, u32[]{:S(2)}) collective-permute-start(bf16[32,4096]{1,0:T(8,128)(2,1)S(1)} %slice.84), channel_id=1, source_target_pairs={{0,192},{64,0},{128,64},{192,128},{1,193},{65,1},{129,65},{193,129... | collective-permute-start | bytes 786440 | tf_op jit(solution)/shard_map/ppermute | solution.py:215
  54.9 0.6 broadcast_in_dim.42.refs_2_
  55.6 0.6 broadcast_in_dim.41.refs_1_
  56.2 0.8 copy.19.refs_3_
  57.0 0.8 slice.97.refs_3_
  57.8 0.6 dynamic_slice.3.refs_0_
  58.4 1.9 %collective-permute-done.5.refs_7_ = bf16[32,4096]{1,0:T(8,128)(2,1)S(1)} collective-permute-done((bf16[32,4096]{1,0:T(8,128)(2,1)S(1)}, bf16[32,4096]{1,0:T(8,128)(2,1)S(1)}, u32[]{:S(2)}, u32[]{:S(2)}) %collective-permute-start.5) | collective-permute-done | bytes 262176 | tf_op jit(solution)/shard_map/ppermute | solution.py:215
  60.3 0.7 copy-done.5
  61.0 0.7 copy-done.6
  61.7 10.3 %scores_lead.1 = (f32[4,256,384]{2,1,0:T(8,128)}, f32[2,384]{1,0:T(2,128)}) custom-call(f32[1]{0:T(128)} %dynamic_slice.3.refs_0_, f32[1,384]{1,0:T(1,128)} %broadcast_in_dim.41.refs_1_, s32[1,384]{1,0:T(1,128)} %broadcast_in_dim.42.refs_2_, s32[256,1]{1,0:T(8,128)} %copy.19.refs_3_, bf16[4,384,4096]{2,1,0:T(8,128)(2,1)} %shift.1.refs_4_.refs_6_, ...), custom_call_target="tpu_custom_call" | custom-call | flops 3221225472 | bytes 16252928 | tf_op jit(solution)/shard_map/scores_lead/pallas_call | solution.py:110
  72.0 11.1 %scores_rest.1 = (f32[4,320,384]{2,1,0:T(8,128)}, f32[2,384]{1,0:T(2,128)}) custom-call(f32[1]{0:T(128)} %dynamic_slice.3.refs_0_, f32[1,384]{1,0:T(1,128)} %broadcast_in_dim.41.refs_1_, s32[1,384]{1,0:T(1,128)} %broadcast_in_dim.42.refs_2_, s32[320,1]{1,0:T(8,128)} %slice.97.refs_3_, bf16[4,384,4096]{2,1,0:T(8,128)(2,1)} %shift.1.refs_4_.refs_6_, ...), custom_call_target="tpu_custom_call" | custom-call | flops 4026531840 | bytes 17170432 | tf_op jit(solution)/shard_map/scores_rest/pallas_call | solution.py:110
  83.1 0.7 broadcast_in_dim.43
  83.8 12.1 %all_to_all.19.refs_1_ = f32[8,2,384]{2,1,0:T(2,128)} all-to-all(f32[8,2,384]{2,1,0:T(2,128)S(1)} %broadcast_in_dim.43), channel_id=1, replica_groups=mesh['x'=4,'z'=8,'y'=4,'c'=2] {'y','c'}, dimensions={0} | all-to-all | bytes 49152 | tf_op jit(solution)/shard_map/all_to_all | solution.py:281
  95.9 13.4 %project.1 = (f32[192,4096]{1,0:T(8,128)}, bf16[96,4096]{1,0:T(8,128)(2,1)}, bf16[96,4096]{1,0:T(8,128)(2,1)}, f32[96,4096]{1,0:T(8,128)}, f32[96,4096]{1,0:T(8,128)}, /*index=5*/f32[1,384]{1,0:T(1,128)}) custom-call(s32[1]{0:T(128)} %bitcast.refs_0_, f32[8,2,384]{2,1,0:T(2,128)} %all_to_all.19.refs_1_, f32[2,384]{1,0:T(2,128)} %get-tuple-element.58.refs_6_.refs_2_, ...), custom_call_target="tpu_custom_call" | custom-call | flops 7247757312 | bytes 25559040 | tf_op jit(solution)/shard_map/project/pallas_call | solution.py:182
  109.3 1.1 copy-done.13
  110.4 2.4 %collective-permute-start.7 = (bf16[96,4096]{1,0:T(8,128)(2,1)S(1)}, bf16[96,4096]{1,0:T(8,128)(2,1)S(1)}, u32[]{:S(2)}, u32[]{:S(2)}) collective-permute-start(bf16[96,4096]{1,0:T(8,128)(2,1)S(1)} %copy-done.13), channel_id=1, source_target_pairs={{0,192},{64,0},{128,64},{192,128},{1,193},{65,1},{129,65},{193,129... | collective-permute-start | bytes 2359304 | tf_op jit(solution)/shard_map/ppermute | solution.py:215
  112.8 16.1 %collective-permute-done.7 = bf16[96,4096]{1,0:T(8,128)(2,1)S(1)} collective-permute-done((bf16[96,4096]{1,0:T(8,128)(2,1)S(1)}, bf16[96,4096]{1,0:T(8,128)(2,1)S(1)}, u32[]{:S(2)}, u32[]{:S(2)}) %collective-permute-start.7) | collective-permute-done | bytes 786464 | tf_op jit(solution)/shard_map/ppermute | solution.py:215
  129.0 3.2 %collective-permute-done.8 = bf16[96,4096]{1,0:T(8,128)(2,1)S(1)} collective-permute-done((bf16[96,4096]{1,0:T(8,128)(2,1)S(1)}, bf16[96,4096]{1,0:T(8,128)(2,1)S(1)}, u32[]{:S(2)}, u32[]{:S(2)}) %collective-permute-start.8) | collective-permute-done | bytes 786464 | tf_op jit(solution)/shard_map/ppermute | solution.py:215
  132.2 0.2 add_convert_fusion.2
  132.4 0.4 collective-permute-start.9
  132.8 1.1 collective-permute-start.10
  133.9 7.4 %collective-permute-done.9 = bf16[48,4096]{1,0:T(8,128)(2,1)S(1)} collective-permute-done((bf16[48,4096]{1,0:T(8,128)(2,1)S(1)}, bf16[48,4096]{1,0:T(8,128)(2,1)S(1)}, u32[]{:S(2)}, u32[]{:S(2)}) %collective-permute-start.9) | collective-permute-done | bytes 393248 | tf_op jit(solution)/shard_map/ppermute | solution.py:215
  141.4 1.5 collective-permute-done.10
  142.9 0.2 add_convert_fusion.1
  143.2 1.4 reshape.86
  144.5 4.1 %all-to-all-start.2 = ((bf16[8,48,1024]{2,1,0:T(8,128)(2,1)}), bf16[8,48,1024]{2,1,0:T(8,128)(2,1)S(1)}, u32[]{:S(2)}, u32[]{:S(2)}) async-start(bf16[8,48,1024]{2,1,0:T(8,128)(2,1)} %reshape.86), calls=%async_computation.2 | async-start | bytes 1572864 | tf_op jit(solution)/shard_map/all_to_all | solution.py:297
  148.6 2.0 %reduce-scatter.2.cloned.1.call-done = f32[24,4096]{1,0:T(8,128)} async-done(((f32[192,4096]{1,0:T(8,128)}), f32[24,4096]{1,0:T(8,128)}) %reduce-scatter.2.cloned.1.call-update) | async-done | bytes 393232 | tf_op jit(solution)/shard_map/reduce_scatter | solution.py:289
  150.7 1.1 fusion.6
  151.8 2.4 %collective-permute-start.11 = (f32[6,4096]{1,0:T(8,128)S(1)}, f32[6,4096]{1,0:T(8,128)S(1)}, u32[]{:S(2)}, u32[]{:S(2)}) collective-permute-start(f32[6,4096]{1,0:T(8,128)S(1)} %get-tuple-element.76), channel_id=1, source_target_pairs={{0,192},{64,0},{128,64},{192,128},{1,193},{65,1},{129,65},{193,129... | collective-permute-start | bytes 294920 | tf_op jit(solution)/shard_map/ppermute | solution.py:215
  154.2 0.7 collective-permute-start.12
  154.9 0.4 collective-permute-start.13
  155.3 14.5 %all-to-all-done.2 = bf16[8,48,1024]{2,1,0:T(8,128)(2,1)S(1)} async-done(((bf16[8,48,1024]{2,1,0:T(8,128)(2,1)}), bf16[8,48,1024]{2,1,0:T(8,128)(2,1)S(1)}, u32[]{:S(2)}, u32[]{:S(2)}) %all-to-all-start.2) | async-done | bytes 786464 | tf_op jit(solution)/shard_map/all_to_all | solution.py:297
  170.1 0.9 fusion.1
  171.1 1.0 broadcast_in_dim.44
  (63 shorter events, 1.2 us)
Async XLA Ops:
  7.2 10.8 %copy-start.7 = (bf16[1,18,4096]{2,1,0:T(8,128)(2,1)S(1)}, bf16[1,18,4096]{2,1,0:T(8,128)(2,1)}, u32[]{:S(2)}) copy-start(bf16[1,18,4096]{2,1,0:T(8,128)(2,1)} %param.8) | copy-start | bytes 442372
  8.1 31.1 %copy-start.8 = (s32[384,4]{0,1:T(4,128)S(1)}, s32[384,4]{0,1:T(4,128)}, u32[]{:S(2)}) copy-start(s32[384,4]{0,1:T(4,128)} %param.9) | copy-start | bytes 18436
  8.9 27.0 %all-to-all-start = ((bf16[8,8,4096]{2,1,0:T(8,128)(2,1)}), bf16[8,8,4096]{2,1,0:T(8,128)(2,1)S(1)}, u32[]{:S(2)}, u32[]{:S(2)}) async-start(bf16[8,8,4096]{2,1,0:T(8,128)(2,1)} %tile.10), calls=%async_computation | async-start | bytes 1048576 | tf_op jit(solution)/shard_map/all_to_all | solution.py:258
  17.9 54.1 %all-gather.2.cloned.1.call-start = ((), (), s32[]{:S(2)}) async-start(), calls=%async_computation.4 | async-start | bytes 2949120 | tf_op jit(solution)/shard_map/all_gather | solution.py:261
  18.0 5.1 %collective-permute-start = (bf16[10,4096]{1,0:T(8,128)(2,1)S(1)}, bf16[10,4096]{1,0:T(8,128)(2,1)S(1)}, u32[]{:S(2)}, u32[]{:S(2)}) collective-permute-start(bf16[10,4096]{1,0:T(8,128)(2,1)S(1)} %slice_bitcast_fusion), channel_id=1, source_target_pairs={{0,64},{64,128},{128,192},{192,0},{1,65},{65,129},{129,193},{193,1... | collective-permute-start | bytes 245768 | tf_op jit(solution)/shard_map/ppermute | solution.py:215
  19.3 7.8 %collective-permute-start.1 = (bf16[10,4096]{1,0:T(8,128)(2,1)S(1)}, bf16[10,4096]{1,0:T(8,128)(2,1)S(1)}, u32[]{:S(2)}, u32[]{:S(2)}) collective-permute-start(bf16[10,4096]{1,0:T(8,128)(2,1)S(1)} %slice_bitcast_fusion), channel_id=1, source_target_pairs={{0,128},{64,192},{128,0},{192,64},{1,129},{65,193},{129,1},{193,65... | collective-permute-start | bytes 245768 | tf_op jit(solution)/shard_map/ppermute | solution.py:215
  21.7 5.5 %collective-permute-start.2 = (bf16[10,4096]{1,0:T(8,128)(2,1)S(1)}, bf16[10,4096]{1,0:T(8,128)(2,1)S(1)}, u32[]{:S(2)}, u32[]{:S(2)}) collective-permute-start(bf16[10,4096]{1,0:T(8,128)(2,1)S(1)} %slice_bitcast_fusion), channel_id=1, source_target_pairs={{0,192},{64,0},{128,64},{192,128},{1,193},{65,1},{129,65},{193,129... | collective-permute-start | bytes 245768 | tf_op jit(solution)/shard_map/ppermute | solution.py:215
  35.9 16.1 %copy-start = (bf16[8,8,4096]{2,1,0:T(8,128)(2,1)}, bf16[8,8,4096]{2,1,0:T(8,128)(2,1)S(1)}, u32[]{:S(2)}) copy-start(bf16[8,8,4096]{2,1,0:T(8,128)(2,1)S(1)} %all-to-all-done) | copy-start | bytes 1572868
  35.9 114.7 %reduce-scatter.2.cloned.1.call-start = ((), (), s32[]{:S(2)}) async-start(), calls=%async_computation.5 | async-start | bytes 3538944 | tf_op jit(solution)/shard_map/reduce_scatter | solution.py:289
  36.0 16.0 %collective-permute-start.3 = (bf16[64,4096]{1,0:T(8,128)(2,1)S(1)}, bf16[64,4096]{1,0:T(8,128)(2,1)S(1)}, u32[]{:S(2)}, u32[]{:S(2)}) collective-permute-start(bf16[64,4096]{1,0:T(8,128)(2,1)S(1)} %bitcast.10), channel_id=1, source_target_pairs={{0,64},{64,128},{128,192},{192,0},{1,65},{65,129},{129,193},{193,1... | collective-permute-start | bytes 1572872 | tf_op jit(solution)/shard_map/ppermute | solution.py:215
  37.3 14.8 %collective-permute-start.4 = (bf16[64,4096]{1,0:T(8,128)(2,1)S(1)}, bf16[64,4096]{1,0:T(8,128)(2,1)S(1)}, u32[]{:S(2)}, u32[]{:S(2)}) collective-permute-start(bf16[64,4096]{1,0:T(8,128)(2,1)S(1)} %bitcast.11), channel_id=1, source_target_pairs={{0,192},{64,0},{128,64},{192,128},{1,193},{65,1},{129,65},{193,129... | collective-permute-start | bytes 1572872 | tf_op jit(solution)/shard_map/ppermute | solution.py:215
  40.0 14.9 %copy-start.9 = (s32[384]{0:T(512)S(1)}, s32[384]{0:T(512)}, u32[]{:S(2)}) copy-start(s32[384]{0:T(512)} %param.11) | copy-start | bytes 4612
  40.0 15.5 %copy-start.10 = (s32[384]{0:T(512)S(1)}, s32[384]{0:T(512)}, u32[]{:S(2)}) copy-start(s32[384]{0:T(512)} %param.10) | copy-start | bytes 4612
  40.0 15.5 %copy-start.11 = (f32[16]{0:T(128)S(1)}, f32[16]{0:T(128)}, u32[]{:S(2)}) copy-start(f32[16]{0:T(128)} %param.12) | copy-start | bytes 196
  40.0 17.8 %copy-start.14 = (f32[4]{0:T(128)S(1)}, f32[4]{0:T(128)}, u32[]{:S(2)}) copy-start(f32[4]{0:T(128)} %param.13) | copy-start | bytes 52
  52.0 8.2 %copy-start.3 = (bf16[64,4096]{1,0:T(8,128)(2,1)}, bf16[64,4096]{1,0:T(8,128)(2,1)S(1)}, u32[]{:S(2)}) copy-start(bf16[64,4096]{1,0:T(8,128)(2,1)S(1)} %collective-permute-done.3.refs_6_) | copy-start | bytes 1572868
  52.1 8.2 %copy-start.4 = (bf16[64,4096]{1,0:T(8,128)(2,1)}, bf16[64,4096]{1,0:T(8,128)(2,1)S(1)}, u32[]{:S(2)}) copy-start(bf16[64,4096]{1,0:T(8,128)(2,1)S(1)} %collective-permute-done.4.refs_9_) | copy-start | bytes 1572868
  52.1 8.1 %collective-permute-start.5 = (bf16[32,4096]{1,0:T(8,128)(2,1)S(1)}, bf16[32,4096]{1,0:T(8,128)(2,1)S(1)}, u32[]{:S(2)}, u32[]{:S(2)}) collective-permute-start(bf16[32,4096]{1,0:T(8,128)(2,1)S(1)} %slice.83), channel_id=1, source_target_pairs={{0,64},{64,128},{128,192},{192,0},{1,65},{65,129},{129,193},{193,1... | collective-permute-start | bytes 786440 | tf_op jit(solution)/shard_map/ppermute | solution.py:215
  52.2 8.0 %collective-permute-start.6 = (bf16[32,4096]{1,0:T(8,128)(2,1)S(1)}, bf16[32,4096]{1,0:T(8,128)(2,1)S(1)}, u32[]{:S(2)}, u32[]{:S(2)}) collective-permute-start(bf16[32,4096]{1,0:T(8,128)(2,1)S(1)} %slice.84), channel_id=1, source_target_pairs={{0,192},{64,0},{128,64},{192,128},{1,193},{65,1},{129,65},{193,129... | collective-permute-start | bytes 786440 | tf_op jit(solution)/shard_map/ppermute | solution.py:215
  60.3 0.7 copy-start.5
  61.0 0.7 copy-start.6
  109.3 1.1 copy-start.13
  109.3 3.6 %copy-start.12 = (bf16[96,4096]{1,0:T(8,128)(2,1)S(1)}, bf16[96,4096]{1,0:T(8,128)(2,1)}, u32[]{:S(2)}) copy-start(bf16[96,4096]{1,0:T(8,128)(2,1)} %get-tuple-element.67) | copy-start | bytes 2359300
  109.3 22.9 %copy-start.1 = (f32[96,4096]{1,0:T(8,128)S(1)}, f32[96,4096]{1,0:T(8,128)}, u32[]{:S(2)}) copy-start(f32[96,4096]{1,0:T(8,128)} %get-tuple-element.69) | copy-start | bytes 4718596
  110.4 18.6 %collective-permute-start.7 = (bf16[96,4096]{1,0:T(8,128)(2,1)S(1)}, bf16[96,4096]{1,0:T(8,128)(2,1)S(1)}, u32[]{:S(2)}, u32[]{:S(2)}) collective-permute-start(bf16[96,4096]{1,0:T(8,128)(2,1)S(1)} %copy-done.13), channel_id=1, source_target_pairs={{0,192},{64,0},{128,64},{192,128},{1,193},{65,1},{129,65},{193,129... | collective-permute-start | bytes 2359304 | tf_op jit(solution)/shard_map/ppermute | solution.py:215
  112.8 19.4 %collective-permute-start.8 = (bf16[96,4096]{1,0:T(8,128)(2,1)S(1)}, bf16[96,4096]{1,0:T(8,128)(2,1)S(1)}, u32[]{:S(2)}, u32[]{:S(2)}) collective-permute-start(bf16[96,4096]{1,0:T(8,128)(2,1)S(1)} %copy-done.12), channel_id=1, source_target_pairs={{0,64},{64,128},{128,192},{192,0},{1,65},{65,129},{129,193},{193,1... | collective-permute-start | bytes 2359304 | tf_op jit(solution)/shard_map/ppermute | solution.py:215
  132.2 10.7 %copy-start.2 = (f32[96,4096]{1,0:T(8,128)S(1)}, f32[96,4096]{1,0:T(8,128)}, u32[]{:S(2)}) copy-start(f32[96,4096]{1,0:T(8,128)} %get-tuple-element.63) | copy-start | bytes 4718596
  132.4 9.0 %collective-permute-start.9 = (bf16[48,4096]{1,0:T(8,128)(2,1)S(1)}, bf16[48,4096]{1,0:T(8,128)(2,1)S(1)}, u32[]{:S(2)}, u32[]{:S(2)}) collective-permute-start(bf16[48,4096]{1,0:T(8,128)(2,1)S(1)} %get-tuple-element.71), channel_id=1, source_target_pairs={{0,192},{64,0},{128,64},{192,128},{1,193},{65,1},{129,65},{193,129... | collective-permute-start | bytes 1179656 | tf_op jit(solution)/shard_map/ppermute | solution.py:215
  132.8 10.1 %collective-permute-start.10 = (bf16[48,4096]{1,0:T(8,128)(2,1)S(1)}, bf16[48,4096]{1,0:T(8,128)(2,1)S(1)}, u32[]{:S(2)}, u32[]{:S(2)}) collective-permute-start(bf16[48,4096]{1,0:T(8,128)(2,1)S(1)} %get-tuple-element.72), channel_id=1, source_target_pairs={{0,64},{64,128},{128,192},{192,0},{1,65},{65,129},{129,193},{193,1... | collective-permute-start | bytes 1179656 | tf_op jit(solution)/shard_map/ppermute | solution.py:215
  144.5 25.3 %all-to-all-start.2 = ((bf16[8,48,1024]{2,1,0:T(8,128)(2,1)}), bf16[8,48,1024]{2,1,0:T(8,128)(2,1)S(1)}, u32[]{:S(2)}, u32[]{:S(2)}) async-start(bf16[8,48,1024]{2,1,0:T(8,128)(2,1)} %reshape.86), calls=%async_computation.2 | async-start | bytes 1572864 | tf_op jit(solution)/shard_map/all_to_all | solution.py:297
  151.8 18.3 %collective-permute-start.11 = (f32[6,4096]{1,0:T(8,128)S(1)}, f32[6,4096]{1,0:T(8,128)S(1)}, u32[]{:S(2)}, u32[]{:S(2)}) collective-permute-start(f32[6,4096]{1,0:T(8,128)S(1)} %get-tuple-element.76), channel_id=1, source_target_pairs={{0,192},{64,0},{128,64},{192,128},{1,193},{65,1},{129,65},{193,129... | collective-permute-start | bytes 294920 | tf_op jit(solution)/shard_map/ppermute | solution.py:215
  154.2 15.9 %collective-permute-start.12 = (f32[6,4096]{1,0:T(8,128)S(1)}, f32[6,4096]{1,0:T(8,128)S(1)}, u32[]{:S(2)}, u32[]{:S(2)}) collective-permute-start(f32[6,4096]{1,0:T(8,128)S(1)} %get-tuple-element.77), channel_id=1, source_target_pairs={{0,128},{64,192},{128,0},{192,64},{1,129},{65,193},{129,1},{193,65... | collective-permute-start | bytes 294920 | tf_op jit(solution)/shard_map/ppermute | solution.py:215
  154.9 15.2 %collective-permute-start.13 = (f32[6,4096]{1,0:T(8,128)S(1)}, f32[6,4096]{1,0:T(8,128)S(1)}, u32[]{:S(2)}, u32[]{:S(2)}) collective-permute-start(f32[6,4096]{1,0:T(8,128)S(1)} %get-tuple-element.78), channel_id=1, source_target_pairs={{0,64},{64,128},{128,192},{192,0},{1,65},{65,129},{129,193},{193,1... | collective-permute-start | bytes 294920 | tf_op jit(solution)/shard_map/ppermute | solution.py:215
Sparse Core Ops, SparseCore 0:
  36.0 35.8 all-gather.1
  109.4 41.1 reduce-scatter.1
